TPU v7x, 32 devices: a whole 2x2x4 slice. The times are simulated.
32 devices in a mesh: dp: 16 (over z, x, core), tensor: 2 (over y).
Axes of the slice: x: 2, y: 2, z: 4, core: 2. Of those that a mesh axis runs over, the one named last changes fastest.
Arguments:
- inputs: bfloat16 [4096, 768], P('dp'), may hold values from -6 to 6
- encoded: bfloat16 [4096, 768], P('dp'), may hold values from -6 to 6
- cotangent: bfloat16 [4096, 768], P('dp'), may hold values from -6 to 6
- buckets: int32 [256, 256], replicated, may hold values from 0 to 31
- gain_self: float32 [768], replicated, may hold values from 0.5 to 1.5
- gain_cross: float32 [768], replicated, may hold values from 0.5 to 1.5
- gain_ffn: float32 [768], replicated, may hold values from 0.5 to 1.5
- bias_table: float32 [32, 12], P(None, 'tensor'), may hold values from -4 to 4
- self_query: bfloat16 [768, 768], P(None, 'tensor'), may hold values from -0.0546875 to 0.0546875
- self_attention_key: bfloat16 [768, 768], P(None, 'tensor'), may hold values from -0.21875 to 0.21875
- self_value: bfloat16 [768, 768], P(None, 'tensor'), may hold values from -0.21875 to 0.21875
- self_out: bfloat16 [768, 768], P('tensor'), may hold values from -0.625 to 0.625
- cross_query: bfloat16 [768, 768], P(None, 'tensor'), may hold values from -0.0546875 to 0.0546875
- cross_key: bfloat16 [768, 768], P(None, 'tensor'), may hold values from -0.21875 to 0.21875
- cross_value: bfloat16 [768, 768], P(None, 'tensor'), may hold values from -0.21875 to 0.21875
- cross_out: bfloat16 [768, 768], P('tensor'), may hold values from -0.625 to 0.625
- ffn_gate: bfloat16 [768, 2048], P(None, 'tensor'), may hold values from -0.21875 to 0.21875
- ffn_up: bfloat16 [768, 2048], P(None, 'tensor'), may hold values from -0.21875 to 0.21875
- ffn_down: bfloat16 [2048, 768], P('tensor'), may hold values from -0.125 to 0.125
Outputs:
- output: bfloat16 [4096, 768], P(('dp', 'tensor'))
- input_grad: float32 [4096, 768], P(('dp', 'tensor'))
- encoder_states_gradient: float32 [4096, 768], P(('dp', 'tensor'))
- gain_self_grad: float32 [768], replicated
- gain_cross_grad: float32 [768], replicated
- gain_ffn_grad: float32 [768], replicated
- bias_table_grad: float32 [32, 12], P(None, 'tensor')
- self_query_grad: float32 [768, 768], P('dp', 'tensor')
- self_key_grad: float32 [768, 768], P('dp', 'tensor')
- self_value_grad: float32 [768, 768], P('dp', 'tensor')
- self_out_grad: float32 [768, 768], P('tensor', 'dp')
- cross_query_grad: float32 [768, 768], P('dp', 'tensor')
- cross_key_grad: float32 [768, 768], P('dp', 'tensor')
- cross_value_grad: float32 [768, 768], P('dp', 'tensor')
- cross_out_grad: float32 [768, 768], P('tensor', 'dp')
- ffn_gate_grad: float32 [768, 2048], P('dp', 'tensor')
- ffn_up_grad: float32 [768, 2048], P('dp', 'tensor')
- ffn_down_grad: float32 [2048, 768], P('tensor', 'dp')
All inputs are finite; a program needn't handle non-finite values.
Results may differ from a plain program's by a relative error of at most 0.035.
Values may be sent and summed in bfloat16 or wider, within the bound.
No kernel may reach another device: no remote copies, remote signals or barrier semaphores. Data moves between devices by JAX's collectives and lax.ppermute only.
A program may use at most 128 MiB of HBM per device.

v0:
```python
import jax
import jax.numpy as jnp
from jax import lax
from jax.sharding import PartitionSpec as P

HD = 64
LEN = 256
ENC = 256


epsilon = 1e-06
masked = -1e30


def rms_apply(hidden, gain):
    scale = lax.rsqrt(jnp.mean(hidden * hidden, axis=-1, keepdims=True) + epsilon)
    return hidden * scale * gain


def glu_apply(gate, up):
    return jax.nn.gelu(gate, approximate=True) * up


def matmul(left, right):
    return jnp.dot(left, right, preferred_element_type=jnp.float32)


def outer_product(left, right):
    return lax.dot_general(
        left, right, (((0,), (0,)), ((), ())), preferred_element_type=jnp.float32
    )


def back_product(left, weight):
    return lax.dot_general(
        left, weight, (((1,), (1,)), ((), ())), preferred_element_type=jnp.float32
    )


def to_heads(rows, length):
    return rows.reshape(rows.shape[0] // length, length, rows.shape[1] // HD, HD)


def to_rows(heads):
    return heads.reshape(heads.shape[0] * heads.shape[1], heads.shape[2] * HD)


def scores_of(query, keys, extra):
    return jnp.einsum("sqhd,skhd->shqk", query, keys, preferred_element_type=jnp.float32) + extra


def attend(query, keys, values, extra):
    scores = scores_of(query, keys, extra)
    top = jnp.max(scores, axis=-1, keepdims=True)
    lse = top + jnp.log(jnp.sum(jnp.exp(scores - top), axis=-1, keepdims=True))
    probs = jnp.exp(scores - lse).astype(jnp.bfloat16)
    mixed = jnp.einsum("shqk,skhd->sqhd", probs, values, preferred_element_type=jnp.float32)
    return (to_rows(mixed.astype(jnp.bfloat16)), lse)


def attend_back(query, keys, values, extra, lse, grad_mixed):
    probs = jnp.exp(scores_of(query, keys, extra) - lse)
    dprob = jnp.einsum("sqhd,skhd->shqk", grad_mixed, values, preferred_element_type=jnp.float32)
    dscore = probs * (dprob - jnp.sum(probs * dprob, axis=-1, keepdims=True))
    score_low = dscore.astype(jnp.bfloat16)
    dquery = jnp.einsum("shqk,skhd->sqhd", score_low, keys, preferred_element_type=jnp.float32)
    dkeys = jnp.einsum("shqk,sqhd->skhd", score_low, query, preferred_element_type=jnp.float32)
    dvalues = jnp.einsum(
        "shqk,sqhd->skhd",
        probs.astype(jnp.bfloat16),
        grad_mixed,
        preferred_element_type=jnp.float32,
    )
    return (
        to_rows(dquery.astype(jnp.bfloat16)),
        to_rows(dkeys.astype(jnp.bfloat16)),
        to_rows(dvalues.astype(jnp.bfloat16)),
        jnp.sum(dscore, axis=0),
    )


def combine_heads(partial_rows):
    return lax.psum_scatter(partial_rows, "tensor", scatter_dimension=0, tiled=True)


def combine_features(partial_rows):
    return lax.psum_scatter(
        partial_rows.astype(jnp.bfloat16), "tensor", scatter_dimension=0, tiled=True
    ).astype(jnp.float32)


def whole_rows(share):
    return lax.all_gather(share, "tensor", axis=0, tiled=True)


def body(
    inputs,
    encoded,
    cotangent,
    buckets,
    gain_self,
    gain_cross,
    gain_ffn,
    bias_table,
    self_query,
    self_attention_key,
    self_value,
    self_out,
    cross_query,
    cross_key,
    cross_value,
    cross_out,
    ffn_gate,
    ffn_up,
    ffn_down,
):
    groups = lax.axis_size("tensor")
    share = inputs.shape[0] // groups
    offset = lax.axis_index("tensor") * share

    def own_rows(rows):
        return lax.dynamic_slice_in_dim(rows, offset, share, 0)

    table_hot = (
        buckets[:, :, None] == jnp.arange(bias_table.shape[0], dtype=jnp.int32)[None, None, :]
    ).astype(jnp.float32)
    bias = jnp.einsum("qkb,bh->hqk", table_hot, bias_table, precision=lax.Precision.HIGHEST)
    row_pos = jnp.arange(LEN, dtype=jnp.int32)[:, None]
    col_pos = jnp.arange(LEN, dtype=jnp.int32)[None, :]
    extra = jnp.where((col_pos <= row_pos)[None], bias, jnp.float32(masked))[None]
    base = inputs.astype(jnp.float32)
    base_share = own_rows(base)
    first_normalized = rms_apply(base, gain_self).astype(jnp.bfloat16)
    q1 = to_heads(matmul(first_normalized, self_query).astype(jnp.bfloat16), LEN)
    k1 = to_heads(matmul(first_normalized, self_attention_key).astype(jnp.bfloat16), LEN)
    v1 = to_heads(matmul(first_normalized, self_value).astype(jnp.bfloat16), LEN)
    mixed1, lse1 = attend(q1, k1, v1, extra)
    first_share = base_share + combine_heads(matmul(mixed1, self_out))
    normed2 = whole_rows(rms_apply(first_share, gain_cross).astype(jnp.bfloat16))
    q2 = to_heads(matmul(normed2, cross_query).astype(jnp.bfloat16), LEN)
    k2 = to_heads(matmul(encoded, cross_key).astype(jnp.bfloat16), ENC)
    v2 = to_heads(matmul(encoded, cross_value).astype(jnp.bfloat16), ENC)
    mixed2, lse2 = attend(q2, k2, v2, jnp.float32(0.0))
    second_share = first_share + combine_heads(matmul(mixed2, cross_out))
    normed3 = whole_rows(rms_apply(second_share, gain_ffn).astype(jnp.bfloat16))
    gate = matmul(normed3, ffn_gate)
    up = matmul(normed3, ffn_up)
    hidden = glu_apply(gate, up).astype(jnp.bfloat16)
    output = (second_share + combine_heads(matmul(hidden, ffn_down))).astype(jnp.bfloat16)
    grad_down = outer_product(hidden, cotangent)
    grad_hidden = back_product(cotangent, ffn_down)
    unused, pull = jax.vjp(glu_apply, gate, up)
    grad_gate, grad_up = pull(grad_hidden)
    grad_gate = grad_gate.astype(jnp.bfloat16)
    grad_up = grad_up.astype(jnp.bfloat16)
    grad_fgate = outer_product(normed3, grad_gate)
    grad_fup = outer_product(normed3, grad_up)
    grad_n3 = combine_features(back_product(grad_gate, ffn_gate) + back_product(grad_up, ffn_up))
    unused, pull = jax.vjp(rms_apply, second_share, gain_ffn)
    back3, grad_gain_ffn = pull(grad_n3)
    grad_second = own_rows(cotangent).astype(jnp.float32) + back3
    second_low = whole_rows(grad_second.astype(jnp.bfloat16))
    grad_cout = outer_product(mixed2, second_low)
    grad_mixed2 = to_heads(back_product(second_low, cross_out).astype(jnp.bfloat16), LEN)
    dq2, dk2, dv2, unused_sum = attend_back(q2, k2, v2, jnp.float32(0.0), lse2, grad_mixed2)
    grad_cquery = outer_product(normed2, dq2)
    grad_ckey = outer_product(encoded, dk2)
    grad_cvalue = outer_product(encoded, dv2)
    second_norm_gradient, grad_encoded = (
        lax.psum_scatter(
            back_product(dq2, cross_query).astype(jnp.bfloat16),
            "tensor",
            scatter_dimension=0,
            tiled=True,
        ).astype(jnp.float32),
        lax.psum_scatter(
            (back_product(dk2, cross_key) + back_product(dv2, cross_value)).astype(jnp.bfloat16),
            "tensor",
            scatter_dimension=0,
            tiled=True,
        ).astype(jnp.float32),
    )
    unused, pull = jax.vjp(rms_apply, first_share, gain_cross)
    back2, grad_gain_cross = pull(second_norm_gradient)
    grad_first = grad_second + back2
    first_low = whole_rows(grad_first.astype(jnp.bfloat16))
    grad_sout = outer_product(mixed1, first_low)
    grad_mixed1 = to_heads(back_product(first_low, self_out).astype(jnp.bfloat16), LEN)
    dq1, self_key_delta, dv1, score_sum = attend_back(q1, k1, v1, extra, lse1, grad_mixed1)
    grad_table = jnp.einsum("hqk,qkb->bh", score_sum, table_hot, precision=lax.Precision.HIGHEST)
    grad_squery = outer_product(first_normalized, dq1)
    self_attention_key_gradient = outer_product(first_normalized, self_key_delta)
    grad_svalue = outer_product(first_normalized, dv1)
    grad_n1 = combine_features(
        back_product(dq1, self_query)
        + back_product(self_key_delta, self_attention_key)
        + back_product(dv1, self_value)
    )
    unused, pull = jax.vjp(rms_apply, base_share, gain_self)
    back1, grad_gain_self = pull(grad_n1)
    input_grad = grad_first + back1
    summed = (
        lax.psum_scatter(grad_squery, "dp", scatter_dimension=0, tiled=True),
        lax.psum_scatter(self_attention_key_gradient, "dp", scatter_dimension=0, tiled=True),
        lax.psum_scatter(grad_svalue, "dp", scatter_dimension=0, tiled=True),
        lax.psum_scatter(grad_sout, "dp", scatter_dimension=1, tiled=True),
        lax.psum_scatter(grad_cquery, "dp", scatter_dimension=0, tiled=True),
        lax.psum_scatter(grad_ckey, "dp", scatter_dimension=0, tiled=True),
        lax.psum_scatter(grad_cvalue, "dp", scatter_dimension=0, tiled=True),
        lax.psum_scatter(grad_cout, "dp", scatter_dimension=1, tiled=True),
        lax.psum_scatter(grad_fgate, "dp", scatter_dimension=0, tiled=True),
        lax.psum_scatter(grad_fup, "dp", scatter_dimension=0, tiled=True),
        lax.psum_scatter(grad_down, "dp", scatter_dimension=1, tiled=True),
    )
    gain_one, gain_two, gain_three = lax.psum(
        (grad_gain_self, grad_gain_cross, grad_gain_ffn), ("dp", "tensor")
    )
    table_total = lax.psum(grad_table, "dp")
    return (
        output,
        input_grad,
        grad_encoded,
        gain_one,
        gain_two,
        gain_three,
        table_total,
        summed[0],
        summed[1],
        summed[2],
        summed[3],
        summed[4],
        summed[5],
        summed[6],
        summed[7],
        summed[8],
        summed[9],
        summed[10],
    )


def solution(mesh):
    in_specs = (
        P("dp", None),
        P("dp", None),
        P("dp", None),
        P(),
        P(),
        P(),
        P(),
        P(None, "tensor"),
        P(None, "tensor"),
        P(None, "tensor"),
        P(None, "tensor"),
        P("tensor", None),
        P(None, "tensor"),
        P(None, "tensor"),
        P(None, "tensor"),
        P("tensor", None),
        P(None, "tensor"),
        P(None, "tensor"),
        P("tensor", None),
    )
    out_specs = (
        P(("dp", "tensor"), None),
        P(("dp", "tensor"), None),
        P(("dp", "tensor"), None),
        P(),
        P(),
        P(),
        P(None, "tensor"),
        P("dp", "tensor"),
        P("dp", "tensor"),
        P("dp", "tensor"),
        P("tensor", "dp"),
        P("dp", "tensor"),
        P("dp", "tensor"),
        P("dp", "tensor"),
        P("tensor", "dp"),
        P("dp", "tensor"),
        P("dp", "tensor"),
        P("tensor", "dp"),
    )
    return jax.shard_map(body, mesh=mesh, in_specs=in_specs, out_specs=out_specs, check_vma=False)
```

profile of v0, /device:TPU:0, one launch (start us, length us, event | category | flops | bytes accessed | tf_op | source)
XLA Modules:
  0.0 902.0 jit_solution(7039383762852925270)
XLA Ops:
  7.9 1.2 multiply_reduce_fusion.2
  9.2 1.7 convolution_convert_fusion.15
  12.8 1.8 copy.91
  16.0 2.7 fusion.1
  18.6 1.9 fusion.51
  22.5 1.3 fusion.53
  24.8 2.3 convolution_convert_fusion.10
  27.1 1.8 copy.98
  28.9 2.1 convolution_convert_fusion.12
  31.0 1.7 copy.96
  32.7 11.5 %reduce-scatter.23.cloned.1.call-done = f32[128,768]{1,0:T(8,128)} async-done(((f32[256,768]{1,0:T(8,128)}), f32[128,768]{1,0:T(8,128)}) %reduce-scatter.23.cloned.1.call-update) | async-done | bytes 393232 | tf_op jit(solution)/shard_map/reduce_scatter | solution.py:83
  44.2 1.9 multiply_reduce_fusion.5
  46.7 7.2 all_gather.12
  55.7 1.7 copy.97
  57.5 1.5 fusion.52
  60.8 1.3 fusion.54
  62.1 17.6 %reduce-scatter.25.cloned.1.call-done = f32[128,768]{1,0:T(8,128)} async-done(((f32[256,768]{1,0:T(8,128)}), f32[128,768]{1,0:T(8,128)}) %reduce-scatter.25.cloned.1.call-update) | async-done | bytes 393232 | tf_op jit(solution)/shard_map/reduce_scatter | solution.py:83
  79.8 1.2 multiply_reduce_fusion.4
  82.6 7.3 all_gather.13
  92.4 2.1 multiply_convert_fusion.1
  95.5 1.4 fusion.5
  97.0 13.3 %reduce-scatter.29.cloned.1.call-done = bf16[128,768]{1,0:T(8,128)(2,1)} async-done(((bf16[256,768]{1,0:T(8,128)(2,1)}), bf16[128,768]{1,0:T(8,128)(2,1)}) %reduce-scatter.29.cloned.1.call-update) | async-done | bytes 196624 | tf_op jit(solution)/shard_map/reduce_scatter | solution.py:87
  110.2 1.9 fusion.29
  113.3 1.3 fusion.41
  114.6 7.1 all_gather.14
  123.6 1.7 copy.100
  125.3 2.2 multiply_reduce_fusion.1
  129.7 1.2 convolution_convert_fusion
  130.9 2.5 fusion.57
  133.5 1.7 convolution_convert_fusion.2
  135.2 1.5 fusion.60
  139.1 5.1 reduce-scatter.31.cloned.1.call-done
  144.2 1.7 fusion.30
  146.4 17.4 %reduce-scatter.27.cloned.1.call-done = f32[128,768]{1,0:T(8,128)} async-done(((f32[256,768]{1,0:T(8,128)}), f32[128,768]{1,0:T(8,128)}) %reduce-scatter.27.cloned.1.call-update) | async-done | bytes 393232 | tf_op jit(solution)/shard_map/reduce_scatter | solution.py:83
  163.9 2.2 fusion.49
  166.1 7.1 all_gather.15
  178.7 1.2 fusion.6
  180.1 1.5 fusion.63
  181.9 1.5 copy.124
  183.5 1.4 fusion.62
  185.6 1.4 copy.122
  187.1 1.5 fusion.61
  188.7 1.5 fusion.46
  190.3 1.5 fusion.47
  191.9 1.5 fusion.48
  193.5 2.3 fusion.66
  196.9 2.3 fusion.65
  200.3 2.3 fusion.64
  203.7 1.7 convert_element_type.226
  205.4 5.5 fusion.10
  210.9 32.9 %psum.31 = f32[32,6]{0,1:T(8,128)} all-reduce(f32[32,6]{0,1:T(8,128)S(1)} %fusion.10), channel_id=1, replica_groups=mesh['dp'=16,'tensor'=2] {'dp'}, use_global_device_ids=true, to_apply=%region_26.27 | all-reduce | flops 192 | bytes 1536 | tf_op jit(solution)/shard_map/psum | solution.py:218
  243.8 1.2 fusion.31
  245.1 37.1 %all-reduce = (f32[768]{0:T(1024)}, f32[768]{0:T(1024)}, f32[768]{0:T(1024)}) all-reduce(f32[768]{0:T(1024)S(1)} %get-tuple-element.72, f32[768]{0:T(1024)S(1)} %copy-done.73, f32[768]{0:T(1024)S(1)} %copy-done.72), channel_id=1, replica_groups=mesh['dp'=16,'tensor'=2] {'dp','tensor'}, use_global_device_ids=true, to_apply=%region_21.22 | all-reduce | flops 2304 | bytes 18432 | tf_op jit(solution)/shard_map/psum | solution.py:215
  282.8 1.9 fusion.34
  284.7 33.7 %reduce-scatter.57.cloned.1.call-done = f32[48,384]{1,0:T(8,128)} async-done(((f32[768,384]{1,0:T(8,128)}), f32[48,384]{1,0:T(8,128)}) %reduce-scatter.57.cloned.1.call-update) | async-done | bytes 73744
  318.4 61.3 %reduce-scatter.45.cloned.1.call-done = f32[48,384]{1,0:T(8,128)} async-done(((f32[768,384]{1,0:T(8,128)}), f32[48,384]{1,0:T(8,128)}) %reduce-scatter.45.cloned.1.call-update) | async-done | bytes 73744 | tf_op jit(solution)/shard_map/reduce_scatter | solution.py:207
  379.7 61.5 %reduce-scatter.55.cloned.1.call-done = f32[48,384]{1,0:T(8,128)} async-done(((f32[768,384]{1,0:T(8,128)}), f32[48,384]{1,0:T(8,128)}) %reduce-scatter.55.cloned.1.call-update) | async-done | bytes 73744
  441.2 61.2 %reduce-scatter.43.cloned.1.call-done = f32[384,48]{0,1:T(8,128)} async-done(((f32[384,768]{0,1:T(8,128)}), f32[384,48]{0,1:T(8,128)}) %reduce-scatter.43.cloned.1.call-update) | async-done | bytes 73744 | tf_op jit(solution)/shard_map/reduce_scatter | solution.py:206
  502.4 61.4 %reduce-scatter.41.cloned.1.call-done = f32[48,384]{1,0:T(8,128)} async-done(((f32[768,384]{1,0:T(8,128)}), f32[48,384]{1,0:T(8,128)}) %reduce-scatter.41.cloned.1.call-update) | async-done | bytes 73744 | tf_op jit(solution)/shard_map/reduce_scatter | solution.py:205
  563.8 61.2 %reduce-scatter.39.cloned.1.call-done = f32[48,384]{1,0:T(8,128)} async-done(((f32[768,384]{1,0:T(8,128)}), f32[48,384]{1,0:T(8,128)}) %reduce-scatter.39.cloned.1.call-update) | async-done | bytes 73744 | tf_op jit(solution)/shard_map/reduce_scatter | solution.py:204
  625.1 61.3 %reduce-scatter.37.cloned.1.call-done = f32[48,384]{1,0:T(8,128)} async-done(((f32[768,384]{1,0:T(8,128)}), f32[48,384]{1,0:T(8,128)}) %reduce-scatter.37.cloned.1.call-update) | async-done | bytes 73744 | tf_op jit(solution)/shard_map/reduce_scatter | solution.py:203
  686.4 69.7 %reduce-scatter.53.cloned.1.call-done = f32[1024,48]{0,1:T(8,128)} async-done(((f32[1024,768]{0,1:T(8,128)}), f32[1024,48]{0,1:T(8,128)}) %reduce-scatter.53.cloned.1.call-update) | async-done | bytes 196624 | tf_op jit(solution)/shard_map/reduce_scatter | solution.py:213
  756.1 69.5 %reduce-scatter.51.cloned.1.call-done = f32[48,1024]{1,0:T(8,128)} async-done(((f32[768,1024]{1,0:T(8,128)}), f32[48,1024]{1,0:T(8,128)}) %reduce-scatter.51.cloned.1.call-update) | async-done | bytes 196624 | tf_op jit(solution)/shard_map/reduce_scatter | solution.py:212
  825.6 69.6 %reduce-scatter.49.cloned.1.call-done = f32[48,1024]{1,0:T(8,128)} async-done(((f32[768,1024]{1,0:T(8,128)}), f32[48,1024]{1,0:T(8,128)}) %reduce-scatter.49.cloned.1.call-update) | async-done | bytes 196624 | tf_op jit(solution)/shard_map/reduce_scatter | solution.py:211
  (247 shorter events, 35.3 us)
Async XLA Ops:
  7.2 84.9 %copy-start = (bf16[1024,768]{1,0:T(8,128)(2,1)S(1)}, bf16[1024,768]{1,0:T(8,128)(2,1)}, u32[]{:S(2)}) copy-start(bf16[1024,768]{1,0:T(8,128)(2,1)} %param.37) | copy-start | bytes 4718596
  7.2 4.5 copy-start.9
  7.2 4.5 copy-start.65
  7.2 4.4 copy-start.60
  7.2 37.0 %reduce-scatter.23.cloned.1.call-start = ((), (), s32[]{:S(2)}) async-start(), calls=%async_computation.18 | async-start | bytes 1179648 | tf_op jit(solution)/shard_map/reduce_scatter | solution.py:83
  9.1 5.4 copy-start.70
  9.1 5.4 copy-start.62
  11.7 4.1 copy-start.64
  12.8 3.2 copy-start.77
  15.9 2.7 copy-start.58
  20.5 2.0 copy-start.24
  23.8 55.9 %reduce-scatter.25.cloned.1.call-start = ((), (), s32[]{:S(2)}) async-start(), calls=%async_computation.19 | async-start | bytes 1179648 | tf_op jit(solution)/shard_map/reduce_scatter | solution.py:83
  24.8 4.0 copy-start.15
  27.1 19.5 %copy-start.68 = (f32[768]{0:T(1024)S(1)}, f32[768]{0:T(1024)}, u32[]{:S(2)}) copy-start(f32[768]{0:T(1024)} %param.24) | copy-start | bytes 9220
  44.2 10.4 %copy-start.26 = (bf16[768,384]{1,0:T(8,128)(2,1)S(1)}, bf16[768,384]{1,0:T(8,128)(2,1)}, u32[]{:S(2)}) copy-start(bf16[768,384]{1,0:T(8,128)(2,1)} %param.31) | copy-start | bytes 1769476
  57.5 1.8 copy-start.48
  59.0 1.8 copy-start.22
  62.1 48.1 %reduce-scatter.29.cloned.1.call-start = ((), (), s32[]{:S(2)}) async-start(), calls=%async_computation.21 | async-start | bytes 589824 | tf_op jit(solution)/shard_map/reduce_scatter | solution.py:87
  79.8 10.1 %copy-start.14 = (bf16[768,1024]{1,0:T(8,128)(2,1)S(1)}, bf16[768,1024]{1,0:T(8,128)(2,1)}, u32[]{:S(2)}) copy-start(bf16[768,1024]{1,0:T(8,128)(2,1)} %param.36) | copy-start | bytes 4718596
  96.9 47.3 %reduce-scatter.31.cloned.1.call-start = ((), (), s32[]{:S(2)}) async-start(), calls=%async_computation.22 | async-start | bytes 589824 | tf_op jit(solution)/shard_map/reduce_scatter | solution.py:170
  110.2 12.3 %copy-start.23 = (bf16[384,768]{1,0:T(8,128)(2,1)S(1)}, bf16[384,768]{1,0:T(8,128)(2,1)}, u32[]{:S(2)}) copy-start(bf16[384,768]{1,0:T(8,128)(2,1)} %param.34) | copy-start | bytes 1769476
  125.3 2.2 copy-start.3
  127.5 2.2 copy-start.27
  130.9 33.0 %reduce-scatter.27.cloned.1.call-start = ((), (), s32[]{:S(2)}) async-start(), calls=%async_computation.20 | async-start | bytes 1179648 | tf_op jit(solution)/shard_map/reduce_scatter | solution.py:83
  133.4 3.3 copy-start.4
  133.5 70.2 %reduce-scatter.35.cloned.1.call-start = ((), (), s32[]{:S(2)}) async-start(), calls=%async_computation.24 | async-start | bytes 589824 | tf_op jit(solution)/shard_map/reduce_scatter | solution.py:176
  133.5 3.3 copy-start.49
  135.2 2.0 copy-start.38
  135.2 2.6 copy-start.28
  137.2 7.0 copy-start.69
  137.2 7.0 copy-start.76
  137.2 8.7 copy-start.81
  137.2 26.6 %copy-start.8 = (f32[128,768]{1,0:T(8,128)S(1)}, f32[128,768]{1,0:T(8,128)}, u32[]{:S(2)}) copy-start(f32[128,768]{1,0:T(8,128)} %copy-done.7) | copy-start | bytes 1179652
  137.3 26.6 %copy-start.40 = (bf16[128,768]{1,0:T(8,128)(2,1)S(1)}, bf16[128,768]{1,0:T(8,128)(2,1)}, u32[]{:S(2)}) copy-start(bf16[128,768]{1,0:T(8,128)(2,1)} %reduce-scatter.29.cloned.1.call-done) | copy-start | bytes 589828
  137.3 26.6 %copy-start.56 = (bf16[256,768]{1,0:T(8,128)(2,1)S(1)}, bf16[256,768]{1,0:T(8,128)(2,1)}, u32[]{:S(2)}) copy-start(bf16[256,768]{1,0:T(8,128)(2,1)} %param.21) | copy-start | bytes 1179652
  137.3 26.6 %copy-start.67 = (f32[768]{0:T(1024)S(1)}, f32[768]{0:T(1024)}, u32[]{:S(2)}) copy-start(f32[768]{0:T(1024)} %param.25) | copy-start | bytes 9220
  139.1 104.8 %reduce-scatter.33.cloned.1.call-start = ((), (), s32[]{:S(2)}) async-start(), calls=%async_computation.23 | async-start | bytes 589824 | tf_op jit(solution)/shard_map/reduce_scatter | solution.py:87
  146.4 26.7 %copy-start.25 = (bf16[384,768]{1,0:T(8,128)(2,1)S(1)}, bf16[384,768]{1,0:T(8,128)(2,1)}, u32[]{:S(2)}) copy-start(bf16[384,768]{1,0:T(8,128)(2,1)} %param.30) | copy-start | bytes 1769476
  174.1 4.1 copy-start.50
  175.5 1.7 copy-start.59
  178.2 1.9 copy-start.21
  178.2 1.9 copy-start.44
  180.0 104.8 %reduce-scatter.47.cloned.1.call-start = ((), (), s32[]{:S(2)}) async-start(), calls=%async_computation.30 | async-start | bytes 1253376 | tf_op jit(solution)/shard_map/reduce_scatter | solution.py:210
  181.5 136.9 %reduce-scatter.57.cloned.1.call-start = ((), (), s32[]{:S(2)}) async-start(), calls=%async_computation.35 | async-start | bytes 1253376
  183.4 1.8 copy-start.39
  183.4 196.3 %reduce-scatter.45.cloned.1.call-start = ((), (), s32[]{:S(2)}) async-start(), calls=%async_computation.29 | async-start | bytes 1253376 | tf_op jit(solution)/shard_map/reduce_scatter | solution.py:207
  185.0 256.2 %reduce-scatter.55.cloned.1.call-start = ((), (), s32[]{:S(2)}) async-start(), calls=%async_computation.34 | async-start | bytes 1253376
  187.0 1.6 copy-start.10
  187.0 1.6 copy-start.51
  187.0 1.6 copy-start.66
  187.1 315.3 %reduce-scatter.43.cloned.1.call-start = ((), (), s32[]{:S(2)}) async-start(), calls=%async_computation.28 | async-start | bytes 1253376 | tf_op jit(solution)/shard_map/reduce_scatter | solution.py:206
  188.6 375.2 %reduce-scatter.41.cloned.1.call-start = ((), (), s32[]{:S(2)}) async-start(), calls=%async_computation.27 | async-start | bytes 1253376 | tf_op jit(solution)/shard_map/reduce_scatter | solution.py:205
  190.2 434.8 %reduce-scatter.39.cloned.1.call-start = ((), (), s32[]{:S(2)}) async-start(), calls=%async_computation.26 | async-start | bytes 1253376 | tf_op jit(solution)/shard_map/reduce_scatter | solution.py:204
  191.9 1.6 copy-start.33
  191.9 1.6 copy-start.57
  191.9 494.5 %reduce-scatter.37.cloned.1.call-start = ((), (), s32[]{:S(2)}) async-start(), calls=%async_computation.25 | async-start | bytes 1253376 | tf_op jit(solution)/shard_map/reduce_scatter | solution.py:203
  193.5 562.6 %reduce-scatter.53.cloned.1.call-start = ((), (), s32[]{:S(2)}) async-start(), calls=%async_computation.33 | async-start | bytes 3342336 | tf_op jit(solution)/shard_map/reduce_scatter | solution.py:213
  195.8 629.8 %reduce-scatter.51.cloned.1.call-start = ((), (), s32[]{:S(2)}) async-start(), calls=%async_computation.32 | async-start | bytes 3342336 | tf_op jit(solution)/shard_map/reduce_scatter | solution.py:212
  199.3 695.9 %reduce-scatter.49.cloned.1.call-start = ((), (), s32[]{:S(2)}) async-start(), calls=%async_computation.31 | async-start | bytes 3342336 | tf_op jit(solution)/shard_map/reduce_scatter | solution.py:211
  202.6 2.8 copy-start.6
  205.4 39.6 %copy-start.72 = (f32[768]{0:T(1024)S(1)}, f32[768]{0:T(1024)}, u32[]{:S(2)}) copy-start(f32[768]{0:T(1024)} %get-tuple-element.74) | copy-start | bytes 9220
  205.4 39.6 %copy-start.73 = (f32[768]{0:T(1024)S(1)}, f32[768]{0:T(1024)}, u32[]{:S(2)}) copy-start(f32[768]{0:T(1024)} %get-tuple-element.76) | copy-start | bytes 9220
  205.4 77.4 %copy-start.54 = (f32[128,768]{1,0:T(8,128)S(1)}, f32[128,768]{1,0:T(8,128)}, u32[]{:S(2)}) copy-start(f32[128,768]{1,0:T(8,128)} %get-tuple-element.82) | copy-start | bytes 1179652
  205.4 689.8 %copy-start.1 = (bf16[1024,768]{1,0:T(8,128)(2,1)S(1)}, bf16[1024,768]{1,0:T(8,128)(2,1)}, u32[]{:S(2)}) copy-start(bf16[1024,768]{1,0:T(8,128)(2,1)} %param.37) | copy-start | bytes 4718596
  (37 other events, 37.4 us)
Sparse Core Ops, SparseCore 0:
  24.0 20.2 reduce-scatter.22
  62.2 17.5 reduce-scatter.24
  97.0 13.1 reduce-scatter.28
  131.0 13.1 reduce-scatter.30
  146.3 17.5 reduce-scatter.26
  166.0 13.1 reduce-scatter.34
  181.4 13.1 reduce-scatter.32
  198.9 58.2 reduce-scatter.46
  261.3 57.0 reduce-scatter.56
  322.5 57.1 reduce-scatter.44
  383.9 57.2 reduce-scatter.54
  445.2 57.1 reduce-scatter.42
  506.6 57.1 reduce-scatter.40
  567.9 57.1 reduce-scatter.38
  629.1 57.2 reduce-scatter.36
  690.6 65.4 reduce-scatter.52
  760.3 65.2 reduce-scatter.50
  829.8 65.3 reduce-scatter.48
where the time goes:
time: 903 us; the launch traced here: 902 us
  waiting for transfers between devices  676 us (75%)
  blocking collectives  98.7 us (11%)
  matrix products  60.9 us (7%)
  local copies, waits for them, and re-layouts  28.4 us (3%)
  other arithmetic  22.1 us (2%)
  between operations  15.2 us (2%)
    unnamed x20, waiting for transfers between devices  95.5 us
    reduce_scatter x1, waiting for transfers between devices, body(): lax.psum_scatter(grad_down, 'dp', scatter_dimension=1, tiled=True)  69.7 us
    reduce_scatter x1, waiting for transfers between devices, body(): lax.psum_scatter(grad_fgate, 'dp', scatter_dimension=0, tiled=True)  69.6 us
    reduce_scatter x1, waiting for transfers between devices, body(): lax.psum_scatter(grad_fup, 'dp', scatter_dimension=0, tiled=True)  69.5 us
    reduce_scatter x1, waiting for transfers between devices, body(): lax.psum_scatter(grad_svalue, 'dp', scatter_dimension=0, tiled=True)  61.4 us
    reduce_scatter x1, waiting for transfers between devices, body(): lax.psum_scatter(grad_squery, 'dp', scatter_dimension=0, tiled=True)  61.3 us
    reduce_scatter x1, waiting for transfers between devices, body(): lax.psum_scatter(grad_cquery, 'dp', scatter_dimension=0, tiled=True)  61.3 us
    reduce_scatter x1, waiting for transfers between devices, body(): lax.psum_scatter(grad_sout, 'dp', scatter_dimension=1, tiled=True)  61.2 us
  transfers between devices with their start and end apart: 18, of which 15 were waited for; matrix products, arithmetic and copies ran while one was open for 6% of the time, Pallas kernels for 0%

commit v1 on v0

v1 whole, which is shorter than its diff:
```python
import jax
import jax.numpy as jnp
from jax import lax
from jax.sharding import PartitionSpec as P

HD = 64
LEN = 256
ENC = 256


epsilon = 1e-06
masked = -1e30


def rms_apply(hidden, gain):
    scale = lax.rsqrt(jnp.mean(hidden * hidden, axis=-1, keepdims=True) + epsilon)
    return hidden * scale * gain


def glu_apply(gate, up):
    return jax.nn.gelu(gate, approximate=True) * up


def matmul(left, right):
    return jnp.dot(left, right, preferred_element_type=jnp.float32)


def outer_product(left, right):
    return lax.dot_general(
        left, right, (((0,), (0,)), ((), ())), preferred_element_type=jnp.float32
    )


def back_product(left, weight):
    return lax.dot_general(
        left, weight, (((1,), (1,)), ((), ())), preferred_element_type=jnp.float32
    )


def to_heads(rows, length):
    return rows.reshape(rows.shape[0] // length, length, rows.shape[1] // HD, HD)


def to_rows(heads):
    return heads.reshape(heads.shape[0] * heads.shape[1], heads.shape[2] * HD)


def scores_of(query, keys, extra):
    return jnp.einsum("sqhd,skhd->shqk", query, keys, preferred_element_type=jnp.float32) + extra


def attend(query, keys, values, extra):
    scores = scores_of(query, keys, extra)
    top = jnp.max(scores, axis=-1, keepdims=True)
    lse = top + jnp.log(jnp.sum(jnp.exp(scores - top), axis=-1, keepdims=True))
    probs = jnp.exp(scores - lse).astype(jnp.bfloat16)
    mixed = jnp.einsum("shqk,skhd->sqhd", probs, values, preferred_element_type=jnp.float32)
    return (to_rows(mixed.astype(jnp.bfloat16)), lse)


def attend_back(query, keys, values, extra, lse, grad_mixed):
    probs = jnp.exp(scores_of(query, keys, extra) - lse)
    dprob = jnp.einsum("sqhd,skhd->shqk", grad_mixed, values, preferred_element_type=jnp.float32)
    dscore = probs * (dprob - jnp.sum(probs * dprob, axis=-1, keepdims=True))
    score_low = dscore.astype(jnp.bfloat16)
    dquery = jnp.einsum("shqk,skhd->sqhd", score_low, keys, preferred_element_type=jnp.float32)
    dkeys = jnp.einsum("shqk,sqhd->skhd", score_low, query, preferred_element_type=jnp.float32)
    dvalues = jnp.einsum(
        "shqk,sqhd->skhd",
        probs.astype(jnp.bfloat16),
        grad_mixed,
        preferred_element_type=jnp.float32,
    )
    return (
        to_rows(dquery.astype(jnp.bfloat16)),
        to_rows(dkeys.astype(jnp.bfloat16)),
        to_rows(dvalues.astype(jnp.bfloat16)),
        jnp.sum(dscore, axis=0),
    )


def flips(size, bit):
    return [(index, index ^ bit) for index in range(size)]


def swap_tensor(value):
    return lax.ppermute(value, "tensor", flips(lax.axis_size("tensor"), 1))


def sum_tensor(partial_rows):
    received = swap_tensor(partial_rows.astype(jnp.bfloat16))
    return partial_rows + received.astype(jnp.float32)


def scatter_tensor(partial_rows):
    halves = partial_rows.reshape(2, partial_rows.shape[0] // 2, partial_rows.shape[1])
    index = lax.axis_index("tensor")
    sent = lax.dynamic_index_in_dim(halves, 1 - index, 0, keepdims=False)
    kept = lax.dynamic_index_in_dim(halves, index, 0, keepdims=False)
    return kept + swap_tensor(sent.astype(jnp.bfloat16)).astype(jnp.float32)


def scatter_dp(partial_grad):
    size = lax.axis_size("dp")
    bits = size.bit_length() - 1
    index = lax.axis_index("dp")
    rows, columns = partial_grad.shape
    held = partial_grad.astype(jnp.bfloat16).reshape((2,) * bits + (rows // size, columns))
    for bit in range(bits):
        axis = bits - 1 - bit
        side = (index >> bit) & 1
        sent = lax.dynamic_index_in_dim(held, 1 - side, axis, keepdims=False)
        kept = lax.dynamic_index_in_dim(held, side, axis, keepdims=False)
        received = lax.ppermute(sent, "dp", flips(size, 1 << bit))
        held = kept.astype(jnp.float32) + received.astype(jnp.float32)
        if bit < bits - 1:
            held = held.astype(jnp.bfloat16)
    return held


def sum_small(gains, table):
    size = lax.axis_size("dp")
    packed = jnp.concatenate([gains.reshape(-1), table.reshape(-1)])
    bit = 1
    while bit < size:
        packed = packed + lax.ppermute(packed, "dp", flips(size, bit))
        bit *= 2
    gains = packed[: gains.size].reshape(gains.shape)
    gains = gains + swap_tensor(gains)
    return gains, packed[gains.size :].reshape(table.shape)


def body(
    inputs,
    encoded,
    cotangent,
    buckets,
    gain_self,
    gain_cross,
    gain_ffn,
    bias_table,
    self_query,
    self_attention_key,
    self_value,
    self_out,
    cross_query,
    cross_key,
    cross_value,
    cross_out,
    ffn_gate,
    ffn_up,
    ffn_down,
):
    groups = lax.axis_size("tensor")
    share = inputs.shape[0] // groups
    offset = lax.axis_index("tensor") * share

    def own_rows(rows):
        return lax.dynamic_slice_in_dim(rows, offset, share, 0)

    table_hot = (
        buckets[:, :, None] == jnp.arange(bias_table.shape[0], dtype=jnp.int32)[None, None, :]
    ).astype(jnp.float32)
    bias = jnp.einsum("qkb,bh->hqk", table_hot, bias_table, precision=lax.Precision.HIGHEST)
    row_pos = jnp.arange(LEN, dtype=jnp.int32)[:, None]
    col_pos = jnp.arange(LEN, dtype=jnp.int32)[None, :]
    extra = jnp.where((col_pos <= row_pos)[None], bias, jnp.float32(masked))[None]
    base = inputs.astype(jnp.float32)
    first_normalized = rms_apply(base, gain_self).astype(jnp.bfloat16)
    q1 = to_heads(matmul(first_normalized, self_query).astype(jnp.bfloat16), LEN)
    k1 = to_heads(matmul(first_normalized, self_attention_key).astype(jnp.bfloat16), LEN)
    v1 = to_heads(matmul(first_normalized, self_value).astype(jnp.bfloat16), LEN)
    mixed1, lse1 = attend(q1, k1, v1, extra)
    first = base + sum_tensor(matmul(mixed1, self_out))
    normed2 = rms_apply(first, gain_cross).astype(jnp.bfloat16)
    q2 = to_heads(matmul(normed2, cross_query).astype(jnp.bfloat16), LEN)
    k2 = to_heads(matmul(encoded, cross_key).astype(jnp.bfloat16), ENC)
    v2 = to_heads(matmul(encoded, cross_value).astype(jnp.bfloat16), ENC)
    mixed2, lse2 = attend(q2, k2, v2, jnp.float32(0.0))
    second = first + sum_tensor(matmul(mixed2, cross_out))
    normed3 = rms_apply(second, gain_ffn).astype(jnp.bfloat16)
    gate = matmul(normed3, ffn_gate)
    up = matmul(normed3, ffn_up)
    hidden = glu_apply(gate, up).astype(jnp.bfloat16)
    grad_hidden = back_product(cotangent, ffn_down)
    unused, pull = jax.vjp(glu_apply, gate, up)
    grad_gate, grad_up = pull(grad_hidden)
    grad_gate = grad_gate.astype(jnp.bfloat16)
    grad_up = grad_up.astype(jnp.bfloat16)
    grad_n3 = sum_tensor(back_product(grad_gate, ffn_gate) + back_product(grad_up, ffn_up))
    ffn_parts = jnp.concatenate(
        [
            outer_product(cotangent, hidden).astype(jnp.bfloat16),
            outer_product(normed3, grad_gate).astype(jnp.bfloat16),
            outer_product(normed3, grad_up).astype(jnp.bfloat16),
        ],
        axis=1,
    )
    ffn_total = scatter_dp(ffn_parts)
    output = (own_rows(second) + scatter_tensor(matmul(hidden, ffn_down))).astype(jnp.bfloat16)
    unused, pull = jax.vjp(rms_apply, second, gain_ffn)
    back3, unused_gain = pull(grad_n3)
    unused, pull_gain = jax.vjp(lambda gain: rms_apply(own_rows(second), gain), gain_ffn)
    (grad_gain_ffn,) = pull_gain(own_rows(grad_n3))
    grad_second = cotangent.astype(jnp.float32) + back3
    second_low = grad_second.astype(jnp.bfloat16)
    grad_mixed2 = to_heads(back_product(second_low, cross_out).astype(jnp.bfloat16), LEN)
    dq2, dk2, dv2, unused_sum = attend_back(q2, k2, v2, jnp.float32(0.0), lse2, grad_mixed2)
    grad_n2 = sum_tensor(back_product(dq2, cross_query))
    cross_parts = jnp.concatenate(
        [
            outer_product(second_low, mixed2).astype(jnp.bfloat16),
            outer_product(normed2, dq2).astype(jnp.bfloat16),
            outer_product(encoded, dk2).astype(jnp.bfloat16),
            outer_product(encoded, dv2).astype(jnp.bfloat16),
        ],
        axis=1,
    )
    cross_total = scatter_dp(cross_parts)
    grad_encoded = scatter_tensor(back_product(dk2, cross_key) + back_product(dv2, cross_value))
    unused, pull = jax.vjp(rms_apply, first, gain_cross)
    back2, unused_gain = pull(grad_n2)
    unused, pull_gain = jax.vjp(lambda gain: rms_apply(own_rows(first), gain), gain_cross)
    (grad_gain_cross,) = pull_gain(own_rows(grad_n2))
    grad_first = grad_second + back2
    first_low = grad_first.astype(jnp.bfloat16)
    grad_mixed1 = to_heads(back_product(first_low, self_out).astype(jnp.bfloat16), LEN)
    dq1, dk1, dv1, score_sum = attend_back(q1, k1, v1, extra, lse1, grad_mixed1)
    self_parts = jnp.concatenate(
        [
            outer_product(first_low, mixed1).astype(jnp.bfloat16),
            outer_product(first_normalized, dq1).astype(jnp.bfloat16),
            outer_product(first_normalized, dk1).astype(jnp.bfloat16),
            outer_product(first_normalized, dv1).astype(jnp.bfloat16),
        ],
        axis=1,
    )
    self_total = scatter_dp(self_parts)
    grad_n1 = scatter_tensor(
        back_product(dq1, self_query)
        + back_product(dk1, self_attention_key)
        + back_product(dv1, self_value)
    )
    unused, pull = jax.vjp(rms_apply, own_rows(base), gain_self)
    back1, grad_gain_self = pull(grad_n1)
    input_grad = own_rows(grad_first) + back1
    grad_table = jnp.einsum("hqk,qkb->bh", score_sum, table_hot, precision=lax.Precision.HIGHEST)
    gains, table_total = sum_small(
        jnp.stack([grad_gain_self, grad_gain_cross, grad_gain_ffn]), grad_table
    )
    units = ffn_gate.shape[1]
    heads = self_query.shape[1]
    return (
        output,
        input_grad,
        grad_encoded,
        gains[0],
        gains[1],
        gains[2],
        table_total,
        self_total[:, heads : 2 * heads],
        self_total[:, 2 * heads : 3 * heads],
        self_total[:, 3 * heads :],
        self_total[:, :heads].T,
        cross_total[:, heads : 2 * heads],
        cross_total[:, 2 * heads : 3 * heads],
        cross_total[:, 3 * heads :],
        cross_total[:, :heads].T,
        ffn_total[:, units : 2 * units],
        ffn_total[:, 2 * units :],
        ffn_total[:, :units].T,
    )


def solution(mesh):
    in_specs = (
        P("dp", None),
        P("dp", None),
        P("dp", None),
        P(),
        P(),
        P(),
        P(),
        P(None, "tensor"),
        P(None, "tensor"),
        P(None, "tensor"),
        P(None, "tensor"),
        P("tensor", None),
        P(None, "tensor"),
        P(None, "tensor"),
        P(None, "tensor"),
        P("tensor", None),
        P(None, "tensor"),
        P(None, "tensor"),
        P("tensor", None),
    )
    out_specs = (
        P(("dp", "tensor"), None),
        P(("dp", "tensor"), None),
        P(("dp", "tensor"), None),
        P(),
        P(),
        P(),
        P(None, "tensor"),
        P("dp", "tensor"),
        P("dp", "tensor"),
        P("dp", "tensor"),
        P("tensor", "dp"),
        P("dp", "tensor"),
        P("dp", "tensor"),
        P("dp", "tensor"),
        P("tensor", "dp"),
        P("dp", "tensor"),
        P("dp", "tensor"),
        P("tensor", "dp"),
    )
    return jax.shard_map(body, mesh=mesh, in_specs=in_specs, out_specs=out_specs, check_vma=False)
```

time: 903 us -> 241 us (0.27)
  waiting for transfers between devices: 676 us -> 81.1 us
  blocking collectives: 98.7 us -> 0 us
  local copies, waits for them, and re-layouts: 28.4 us -> 54.4 us
  starting transfers between devices: 0.97 us -> 25.1 us
  matrix products: 60.9 us -> 44.9 us
  between operations: 15.2 us -> 1.9 us
  other arithmetic: 22.1 us -> 32.8 us
    reduce_scatter x16 -> x0, waiting for transfers between devices: 580 us -> none  [the longest x1 69.7 us: body(): lax.psum_scatter(grad_down, 'dp', scatter_dimension=1, tiled=True)]
    unnamed x20 -> x0, waiting for transfers between devices: 95.5 us -> none
    ppermute x0 -> x24, waiting for transfers between devices: none -> 81.1 us  [the longest x12 64.3 us: scatter_dp(): received = lax.ppermute(sent, 'dp', flips(size, 1 << bit))]
    psum x2 -> x0, blocking collectives: 70 us -> none  [the longest x1 37.1 us: body(): lax.psum((grad_gain_self, grad_gain_cross, grad_gain_ffn), ('dp', 'tensor'))]
    all_gather x4 -> x0, blocking collectives: 28.7 us -> none  [whole_rows(): return lax.all_gather(share, 'tensor', axis=0, tiled=True)]
    ppermute x0 -> x24, starting transfers between devices: none -> 25.1 us  [the longest x12 11.3 us: scatter_dp(): received = lax.ppermute(sent, 'dp', flips(size, 1 << bit))]
    concatenate x0 -> x4, local copies, waits for them, and re-layouts: none -> 14.7 us  [the longest x1 6.63 us: body(): jnp.concatenate([outer_product(cotangent, hidden).astype(jnp.bfloat16), o...]
  transfers between devices with their start and end apart: 18 -> 24, of which waited for: 15 -> 12; matrix products, arithmetic and copies ran while one was open for 6% -> 38% of each run, Pallas kernels for 0% -> 0%
where the time goes in v1:
time: 241 us; the launch traced here: 240 us
  waiting for transfers between devices  81.1 us (34%)
  local copies, waits for them, and re-layouts  54.4 us (23%)
  matrix products  44.9 us (19%)
  other arithmetic  32.8 us (14%)
  starting transfers between devices  25.1 us (10%)
    ppermute x12, waiting for transfers between devices, scatter_dp(): received = lax.ppermute(sent, 'dp', flips(size, 1 << bit))  64.3 us
    ppermute x8, waiting for transfers between devices, swap_tensor(): return lax.ppermute(value, 'tensor', flips(lax.axis_size('tensor'), 1))  14.7 us
    unnamed x197, local copies, waits for them, and re-layouts  14.6 us
    ppermute x12, starting transfers between devices, scatter_dp(): received = lax.ppermute(sent, 'dp', flips(size, 1 << bit))  11.3 us
    dot_general x11, matrix products, matmul(): return jnp.dot(left, right, preferred_element_type=jnp.float32)  10.7 us
    dot_general x11, matrix products, back_product(): lax.dot_general(left, weight, (((1,), (1,)), ((), ())), preferred_element...  10.3 us
    dot_general x11, matrix products, outer_product(): lax.dot_general(left, right, (((0,), (0,)), ((), ())), preferred_element_...  9.29 us
    squeeze x12, local copies, waits for them, and re-layouts, scatter_dp(): sent = lax.dynamic_index_in_dim(held, 1 - side, axis, keepdims=False)  8.72 us
  transfers between devices with their start and end apart: 24, of which 12 were waited for; matrix products, arithmetic and copies ran while one was open for 38% of the time, Pallas kernels for 0%

profile of v1, /device:TPU:0, one launch (start us, length us, event | category | flops | bytes accessed | tf_op | source)
XLA Modules:
  0.0 240.1 jit_solution(13306242605302256851)
XLA Ops:
  1.4 1.2 multiply_reduce_fusion.6
  2.6 1.6 convolution_convert_fusion.26
  7.3 1.7 copy.74
  10.3 2.7 %fusion.1 = f32[256,256,6]{0,2,1:T(8,128)S(1)} fusion(s32[256,256]{0,1:T(8,128)S(1)} %copy.76, f32[32,6]{0,1:T(8,128)S(1)} %copy-done.91), kind=kOutput, calls=%fused_computation.2 | convolution fusion | flops 153092096 | bytes 1835776 | tf_op jit(solution)/shard_map/qkb,bh->hqk/dot_general | solution.py:164
  15.2 1.4 fusion.52
  16.6 3.0 %collective-permute-start = (bf16[256,768]{1,0:T(8,128)(2,1)}, bf16[256,768]{1,0:T(8,128)(2,1)}, u32[]{:S(2)}, u32[]{:S(2)}) collective-permute-start(bf16[256,768]{1,0:T(8,128)(2,1)} %get-tuple-element.67), channel_id=1, source_target_pairs={{0,1},{1,0},{2,3},{3,2},{4,5},{5,4},{6,7},{7,6},{8,9},{9,8},{10,11... | collective-permute-start | bytes 1179656 | tf_op jit(solution)/shard_map/ppermute | solution.py:87
  22.7 1.7 copy.80
  24.5 1.7 copy.82
  26.2 1.6 multiply_reduce_fusion.13
  27.8 3.2 %fusion.59 = f32[256,1024]{1,0:T(8,128)} fusion(bf16[256,768]{1,0:T(8,128)(2,1)} %param.21, bf16[1024,768]{1,0:T(8,128)(2,1)} %param.37), kind=kOutput, calls=%fused_computation.176 | convolution fusion | flops 402653184 | bytes 3014656 | tf_op jit(solution)/shard_map/dot_general | solution.py:35
  31.0 1.3 multiply_reduce_fusion.5
  34.5 1.7 copy.81
  36.3 1.5 fusion.53
  40.9 9.4 %collective-permute-done.1 = bf16[256,768]{1,0:T(8,128)(2,1)S(1)} collective-permute-done((bf16[256,768]{1,0:T(8,128)(2,1)S(1)}, bf16[256,768]{1,0:T(8,128)(2,1)S(1)}, u32[]{:S(2)}, u32[]{:S(2)}) %collective-permute-start.1) | collective-permute-done | bytes 393248 | tf_op jit(solution)/shard_map/ppermute | solution.py:87
  53.2 1.4 multiply_convert_fusion.1
  58.5 1.6 fusion.55
  61.1 1.7 collective-permute-start.2
  62.9 2.4 %pad_maximum_fusion = bf16[768,3072]{0,1:T(8,128)(2,1)} fusion(bf16[768,1024]{0,1:T(8,128)(2,1)S(1)} %convolution_convert_fusion, bf16[768,1024]{0,1:T(8,128)(2,1)S(1)} %convolution_convert_fusion.1, bf16[768,1024]{0,1:T(8,128)(2,1)S(1)} %fusion.9), kind=kLoop, calls=%fused_computation.3 | loop fusion | flops 14155776 | bytes 9437184 | tf_op jit(solution)/shard_map/concatenate | solution.py:191
  65.3 6.6 %copy.98 = bf16[768,3072]{1,0:T(8,128)(2,1)} copy(bf16[768,3072]{0,1:T(8,128)(2,1)} %pad_maximum_fusion) | data formatting | bytes 9437184 | tf_op jit(solution)/shard_map/concatenate | solution.py:191
  71.9 3.3 %dynamic-slice_bitcast_fusion = bf16[2,2,2,48,3072]{4,3,2,1,0:T(8,128)(2,1)} fusion(bf16[2,2,2,2,48,3072]{5,4,3,2,1,0:T(8,128)(2,1)} %bitcast.228, s32[]{:T(128)S(6)} %select_n.81), kind=kLoop, calls=%fused_computation.16 | loop fusion | bytes 4718596 | tf_op jit(solution)/shard_map/jit(dynamic_index_in_dim)/squeeze | solution.py:112
  75.9 1.2 multiply_reduce_fusion.3
  80.3 1.7 copy.84
  82.0 1.5 multiply_reduce_fusion.1
  85.8 1.4 fusion.56
  90.3 1.7 collective-permute-start.6
  92.4 1.7 multiply_reduce_fusion.7
  94.1 1.5 pad_maximum_fusion.2
  95.6 4.3 %copy.95 = bf16[768,1536]{1,0:T(8,128)(2,1)} copy(bf16[768,1536]{0,1:T(8,128)(2,1)} %pad_maximum_fusion.2) | data formatting | bytes 4718592 | tf_op jit(solution)/shard_map/concatenate | solution.py:210
  99.9 2.5 %dynamic-slice_bitcast_fusion.2 = bf16[2,2,2,48,1536]{4,3,2,1,0:T(8,128)(2,1)} fusion(bf16[2,2,2,2,48,1536]{5,4,3,2,1,0:T(8,128)(2,1)} %bitcast.230, s32[]{:T(128)S(6)} %select_n.81), kind=kLoop, calls=%fused_computation.59 | loop fusion | bytes 2359300 | tf_op jit(solution)/shard_map/jit(dynamic_index_in_dim)/squeeze | solution.py:112
  102.5 1.7 collective-permute-done.6
  104.1 1.7 bitcast_add_fusion.1
  105.9 1.2 multiply_reduce_fusion.2
  113.2 5.0 %fusion.17 = f32[32,6]{1,0:T(8,128)} fusion(f32[6,256,256]{1,2,0:T(8,128)S(1)} %subtract_multiply_fusion, s32[256,256]{0,1:T(8,128)S(1)} %copy-done.66), kind=kOutput, calls=%fused_computation.77 | convolution fusion | flops 153092096 | bytes 1835776 | tf_op jit(solution)/shard_map/hqk,qkb->bh/dot_general | solution.py:247
  118.2 1.1 convolution_convert_fusion.8
  119.8 1.3 convolution_convert_fusion.5
  123.9 2.2 convolution_convert_fusion.6
  126.1 3.3 %collective-permute-done.5 = bf16[128,768]{1,0:T(8,128)(2,1)} collective-permute-done((bf16[128,768]{1,0:T(8,128)(2,1)}, bf16[128,768]{1,0:T(8,128)(2,1)}, u32[]{:S(2)}, u32[]{:S(2)}) %collective-permute-start.5) | collective-permute-done | bytes 196640 | tf_op jit(solution)/shard_map/ppermute | solution.py:87
  129.4 1.3 multiply_reduce_fusion.11
  130.7 1.4 constant_dynamic-update-slice_fusion.1
  132.1 1.3 constant_dynamic-update-slice_fusion
  133.4 1.3 convolution_convert_fusion.7
  135.5 1.5 collective-permute-start.8
  137.0 1.4 pad_maximum_fusion.1
  138.4 2.4 %copy.94 = bf16[768,1536]{1,0:T(8,128)(2,1)} copy(bf16[768,1536]{0,1:T(8,128)(2,1)S(1)} %pad_maximum_fusion.1) | data formatting | bytes 4718592 | tf_op jit(solution)/shard_map/concatenate | solution.py:229
  140.8 1.6 collective-permute-start.9
  142.5 2.5 %dynamic-slice_bitcast_fusion.3 = bf16[2,2,2,48,1536]{4,3,2,1,0:T(8,128)(2,1)} fusion(bf16[2,2,2,2,48,1536]{5,4,3,2,1,0:T(8,128)(2,1)} %bitcast.232, s32[]{:T(128)S(6)} %select_n.81), kind=kLoop, calls=%fused_computation.60 | loop fusion | bytes 2359300 | tf_op jit(solution)/shard_map/jit(dynamic_index_in_dim)/squeeze | solution.py:112
  145.0 2.6 %collective-permute-start.10 = (f32[2496]{0:T(1024)S(1)}, f32[2496]{0:T(1024)S(1)}, u32[]{:S(2)}, u32[]{:S(2)}) collective-permute-start(f32[2496]{0:T(1024)S(1)} %add.294), channel_id=1, source_target_pairs={{0,16},{2,18},{4,20},{6,22},{8,24},{10,26},{12,28},{14,30},{16,0},... | collective-permute-start | bytes 29960 | tf_op jit(solution)/shard_map/ppermute | solution.py:126
  147.6 2.0 collective-permute-done.10
  150.2 2.1 fusion.31
  154.1 1.7 fusion.6
  156.4 1.6 fusion.7
  158.1 1.6 collective-permute-start.13
  159.6 12.5 %collective-permute-done.17 = bf16[2,2,48,1536]{3,2,1,0:T(8,128)(2,1)S(1)} collective-permute-done((bf16[2,2,48,1536]{3,2,1,0:T(8,128)(2,1)S(1)}, bf16[2,2,48,1536]{3,2,1,0:T(8,128)(2,1)S(1)}, u32[]{:S(2)}, u32[]{:S(2)}) %collective-permute-start.17) | collective-permute-done | bytes 589856 | tf_op jit(solution)/shard_map/ppermute | solution.py:114
  172.3 1.2 collective-permute-start.18
  173.5 3.3 %fusion.2 = bf16[2,2,2,48,3072]{4,3,2,1,0:T(8,128)(2,1)S(1)} fusion(bf16[2,2,2,48,3072]{4,3,2,1,0:T(8,128)(2,1)} %collective-permute-done.20, bf16[2,2,2,2,48,3072]{5,4,3,2,1,0:T(8,128)(2,1)} %bitcast.229, s32[]{:T(128)S(6)} %select_n.80), kind=kLoop, calls=%fused_computation.5 | loop fusion | flops 4718592 | bytes 7077892 | tf_op jit(solution)/shard_map/convert_element_type | solution.py:117
  177.5 3.2 %collective-permute-done.18 = bf16[2,48,1536]{2,1,0:T(8,128)(2,1)S(1)} collective-permute-done((bf16[2,48,1536]{2,1,0:T(8,128)(2,1)S(1)}, bf16[2,48,1536]{2,1,0:T(8,128)(2,1)S(1)}, u32[]{:S(2)}, u32[]{:S(2)}) %collective-permute-start.18) | collective-permute-done | bytes 294944 | tf_op jit(solution)/shard_map/ppermute | solution.py:114
  180.8 1.9 collective-permute-start.19
  182.7 2.0 collective-permute-done.13
  184.9 1.2 collective-permute-start.14
  186.1 2.1 collective-permute-done.19
  189.0 18.8 %collective-permute-done.21 = bf16[2,2,48,3072]{3,2,1,0:T(8,128)(2,1)S(1)} collective-permute-done((bf16[2,2,48,3072]{3,2,1,0:T(8,128)(2,1)S(1)}, bf16[2,2,48,3072]{3,2,1,0:T(8,128)(2,1)S(1)}, u32[]{:S(2)}, u32[]{:S(2)}) %collective-permute-start.21) | collective-permute-done | bytes 1179680 | tf_op jit(solution)/shard_map/ppermute | solution.py:114
  208.9 2.7 %collective-permute-start.15 = (bf16[48,1536]{1,0:T(8,128)(2,1)S(1)}, bf16[48,1536]{1,0:T(8,128)(2,1)S(1)}, u32[]{:S(2)}, u32[]{:S(2)}) collective-permute-start(bf16[48,1536]{1,0:T(8,128)(2,1)S(1)} %dynamic-slice_bitcast_fusion.11), channel_id=1, source_target_pairs={{0,16},{2,18},{4,20},{6,22},{8,24},{10,26},{12,28},{14,30},{16,0},... | collective-permute-start | bytes 442376 | tf_op jit(solution)/shard_map/ppermute | solution.py:114
  211.5 13.1 %collective-permute-done.22 = bf16[2,48,3072]{2,1,0:T(8,128)(2,1)S(1)} collective-permute-done((bf16[2,48,3072]{2,1,0:T(8,128)(2,1)S(1)}, bf16[2,48,3072]{2,1,0:T(8,128)(2,1)S(1)}, u32[]{:S(2)}, u32[]{:S(2)}) %collective-permute-start.22) | collective-permute-done | bytes 589856 | tf_op jit(solution)/shard_map/ppermute | solution.py:114
  226.6 12.6 %collective-permute-done.23 = bf16[48,3072]{1,0:T(8,128)(2,1)S(1)} collective-permute-done((bf16[48,3072]{1,0:T(8,128)(2,1)S(1)}, bf16[48,3072]{1,0:T(8,128)(2,1)S(1)}, u32[]{:S(2)}, u32[]{:S(2)}) %collective-permute-start.23) | collective-permute-done | bytes 294944 | tf_op jit(solution)/shard_map/ppermute | solution.py:114
  (322 shorter events, 51.3 us)
Async XLA Ops:
  0.7 51.9 %copy-start = (bf16[768,1024]{1,0:T(8,128)(2,1)S(1)}, bf16[768,1024]{1,0:T(8,128)(2,1)}, u32[]{:S(2)}) copy-start(bf16[768,1024]{1,0:T(8,128)(2,1)} %param.35) | copy-start | bytes 4718596
  0.7 5.5 %copy-start.11 = (bf16[256,768]{1,0:T(8,128)(2,1)S(1)}, bf16[256,768]{1,0:T(8,128)(2,1)}, u32[]{:S(2)}) copy-start(bf16[256,768]{1,0:T(8,128)(2,1)} %param.19) | copy-start | bytes 1179652
  0.7 5.5 %copy-start.73 = (f32[768]{0:T(1024)S(1)}, f32[768]{0:T(1024)}, u32[]{:S(2)}) copy-start(f32[768]{0:T(1024)} %param.23) | copy-start | bytes 9220
  0.7 5.4 %copy-start.67 = (bf16[768,384]{1,0:T(8,128)(2,1)S(1)}, bf16[768,384]{1,0:T(8,128)(2,1)}, u32[]{:S(2)}) copy-start(bf16[768,384]{1,0:T(8,128)(2,1)} %param.27) | copy-start | bytes 1769476
  2.6 6.5 %copy-start.83 = (f32[256]{0:T(256)}, f32[256]{0:T(256)S(1)}, u32[]{:S(2)}) copy-start(f32[256]{0:T(256)S(1)} %add_rsqrt_fusion) | copy-start | bytes 3076
  4.2 4.8 %copy-start.69 = (bf16[768,384]{1,0:T(8,128)(2,1)S(1)}, bf16[768,384]{1,0:T(8,128)(2,1)}, u32[]{:S(2)}) copy-start(bf16[768,384]{1,0:T(8,128)(2,1)} %param.28) | copy-start | bytes 1769476
  6.2 4.1 %copy-start.65 = (s32[256,256]{0,1:T(8,128)}, s32[256,256]{0,1:T(8,128)S(1)}, u32[]{:S(2)}) copy-start(s32[256,256]{0,1:T(8,128)S(1)} %copy.76) | copy-start | bytes 786436
  6.2 4.1 %copy-start.91 = (f32[32,6]{0,1:T(8,128)S(1)}, f32[32,6]{0,1:T(8,128)}, u32[]{:S(2)}) copy-start(f32[32,6]{0,1:T(8,128)} %param.26) | copy-start | bytes 2308
  14.8 4.8 %copy-start.20 = (bf16[256,768]{1,0:T(8,128)(2,1)S(1)}, bf16[256,768]{1,0:T(8,128)(2,1)}, u32[]{:S(2)}) copy-start(bf16[256,768]{1,0:T(8,128)(2,1)} %param.20) | copy-start | bytes 1179652
  14.8 4.8 %copy-start.44 = (bf16[768,384]{1,0:T(8,128)(2,1)S(1)}, bf16[768,384]{1,0:T(8,128)(2,1)}, u32[]{:S(2)}) copy-start(bf16[768,384]{1,0:T(8,128)(2,1)} %param.33) | copy-start | bytes 1769476
  15.2 5.5 %copy-start.60 = (bf16[6,64,256]{2,1,0:T(8,128)(2,1)}, bf16[6,64,256]{2,1,0:T(8,128)(2,1)S(1)}, u32[]{:S(2)}) copy-start(bf16[6,64,256]{2,1,0:T(8,128)(2,1)S(1)} %convolution_convert_fusion.23) | copy-start | bytes 589828
  15.2 5.5 %copy-start.38 = (bf16[768,384]{1,0:T(8,128)(2,1)S(1)}, bf16[768,384]{1,0:T(8,128)(2,1)}, u32[]{:S(2)}) copy-start(bf16[768,384]{1,0:T(8,128)(2,1)} %param.32) | copy-start | bytes 1769476
  16.6 14.4 %collective-permute-start = (bf16[256,768]{1,0:T(8,128)(2,1)}, bf16[256,768]{1,0:T(8,128)(2,1)}, u32[]{:S(2)}, u32[]{:S(2)}) collective-permute-start(bf16[256,768]{1,0:T(8,128)(2,1)} %get-tuple-element.67), channel_id=1, source_target_pairs={{0,1},{1,0},{2,3},{3,2},{4,5},{5,4},{6,7},{7,6},{8,9},{9,8},{10,11... | collective-permute-start | bytes 1179656 | tf_op jit(solution)/shard_map/ppermute | solution.py:87
  27.8 3.2 %copy-start.30 = (f32[256,768]{1,0:T(8,128)S(1)}, f32[256,768]{1,0:T(8,128)}, u32[]{:S(2)}) copy-start(f32[256,768]{1,0:T(8,128)} %get-tuple-element.68) | copy-start | bytes 2359300
  38.9 11.4 %copy-start.62 = (bf16[6,64,256]{2,1,0:T(8,128)(2,1)}, bf16[6,64,256]{2,1,0:T(8,128)(2,1)S(1)}, u32[]{:S(2)}) copy-start(bf16[6,64,256]{2,1,0:T(8,128)(2,1)S(1)} %convolution_convert_fusion.19) | copy-start | bytes 589828
  39.7 10.6 %collective-permute-start.1 = (bf16[256,768]{1,0:T(8,128)(2,1)S(1)}, bf16[256,768]{1,0:T(8,128)(2,1)S(1)}, u32[]{:S(2)}, u32[]{:S(2)}) collective-permute-start(bf16[256,768]{1,0:T(8,128)(2,1)S(1)} %get-tuple-element.71), channel_id=1, source_target_pairs={{0,1},{1,0},{2,3},{3,2},{4,5},{5,4},{6,7},{7,6},{8,9},{9,8},{10,11... | collective-permute-start | bytes 1179656 | tf_op jit(solution)/shard_map/ppermute | solution.py:87
  40.3 11.2 %copy-start.78 = (f32[768]{0:T(1024)S(1)}, f32[768]{0:T(1024)}, u32[]{:S(2)}) copy-start(f32[768]{0:T(1024)} %param.25) | copy-start | bytes 9220
  57.2 3.2 %copy-start.35 = (f32[256,768]{1,0:T(8,128)}, f32[256,768]{1,0:T(8,128)S(1)}, u32[]{:S(2)}) copy-start(f32[256,768]{1,0:T(8,128)S(1)} %fusion.58) | copy-start | bytes 2359300
  60.1 15.8 %collective-permute-start.3 = (bf16[256,768]{1,0:T(8,128)(2,1)}, bf16[256,768]{1,0:T(8,128)(2,1)}, u32[]{:S(2)}, u32[]{:S(2)}) collective-permute-start(bf16[256,768]{1,0:T(8,128)(2,1)} %get-tuple-element.73), channel_id=1, source_target_pairs={{0,1},{1,0},{2,3},{3,2},{4,5},{5,4},{6,7},{7,6},{8,9},{9,8},{10,11... | collective-permute-start | bytes 1179656 | tf_op jit(solution)/shard_map/ppermute | solution.py:87
  61.1 31.2 %collective-permute-start.2 = (bf16[128,768]{1,0:T(8,128)(2,1)}, bf16[128,768]{1,0:T(8,128)(2,1)}, u32[]{:S(2)}, u32[]{:S(2)}) collective-permute-start(bf16[128,768]{1,0:T(8,128)(2,1)} %fusion.40), channel_id=1, source_target_pairs={{0,1},{1,0},{2,3},{3,2},{4,5},{5,4},{6,7},{7,6},{8,9},{9,8},{10,11... | collective-permute-start | bytes 589832 | tf_op jit(solution)/shard_map/ppermute | solution.py:87
  71.9 3.4 %copy-start.9 = (f32[256,768]{1,0:T(8,128)S(1)}, f32[256,768]{1,0:T(8,128)}, u32[]{:S(2)}) copy-start(f32[256,768]{1,0:T(8,128)} %copy-done.8) | copy-start | bytes 2359300
  71.9 4.0 %copy-start.32 = (f32[256,768]{1,0:T(8,128)S(1)}, f32[256,768]{1,0:T(8,128)}, u32[]{:S(2)}) copy-start(f32[256,768]{1,0:T(8,128)} %get-tuple-element.74) | copy-start | bytes 2359300
  71.9 4.0 %copy-start.79 = (f32[768]{0:T(1024)S(1)}, f32[768]{0:T(1024)}, u32[]{:S(2)}) copy-start(f32[768]{0:T(1024)} %param.25) | copy-start | bytes 9220
  75.2 2.8 %copy-start.29 = (bf16[256,768]{1,0:T(8,128)(2,1)S(1)}, bf16[256,768]{1,0:T(8,128)(2,1)}, u32[]{:S(2)}) copy-start(bf16[256,768]{1,0:T(8,128)(2,1)} %param.21) | copy-start | bytes 1179652
  75.2 2.8 %copy-start.90 = (f32[256]{0:T(256)S(1)}, f32[256]{0:T(256)}, u32[]{:S(2)}) copy-start(f32[256]{0:T(256)} %copy-done.89) | copy-start | bytes 3076
  75.3 98.2 %collective-permute-start.20 = (bf16[2,2,2,48,3072]{4,3,2,1,0:T(8,128)(2,1)}, bf16[2,2,2,48,3072]{4,3,2,1,0:T(8,128)(2,1)}, u32[]{:S(2)}, u32[]{:S(2)}) collective-permute-start(bf16[2,2,2,48,3072]{4,3,2,1,0:T(8,128)(2,1)} %dynamic-slice_bitcast_fusion), channel_id=1, source_target_pairs={{0,2},{2,0},{4,6},{6,4},{8,10},{10,8},{12,14},{14,12},{16,18},{18,... | collective-permute-start | bytes 7077896 | tf_op jit(solution)/shard_map/ppermute | solution.py:114
  88.0 17.8 %collective-permute-start.4 = (bf16[256,768]{1,0:T(8,128)(2,1)}, bf16[256,768]{1,0:T(8,128)(2,1)}, u32[]{:S(2)}, u32[]{:S(2)}) collective-permute-start(bf16[256,768]{1,0:T(8,128)(2,1)} %get-tuple-element.77), channel_id=1, source_target_pairs={{0,1},{1,0},{2,3},{3,2},{4,5},{5,4},{6,7},{7,6},{8,9},{9,8},{10,11... | collective-permute-start | bytes 1179656 | tf_op jit(solution)/shard_map/ppermute | solution.py:87
  89.2 3.2 %copy-start.10 = (f32[256,768]{1,0:T(8,128)S(1)}, f32[256,768]{1,0:T(8,128)}, u32[]{:S(2)}) copy-start(f32[256,768]{1,0:T(8,128)} %copy-done.8) | copy-start | bytes 2359300
  89.2 3.2 %copy-start.26 = (f32[256,768]{1,0:T(8,128)S(1)}, f32[256,768]{1,0:T(8,128)}, u32[]{:S(2)}) copy-start(f32[256,768]{1,0:T(8,128)} %copy-done.25) | copy-start | bytes 2359300
  89.2 3.2 %copy-start.36 = (f32[256,768]{1,0:T(8,128)S(1)}, f32[256,768]{1,0:T(8,128)}, u32[]{:S(2)}) copy-start(f32[256,768]{1,0:T(8,128)} %copy-done.35) | copy-start | bytes 2359300
  89.2 3.2 %copy-start.93 = (f32[128]{0:T(128)S(1)}, f32[128]{0:T(128)}, u32[]{:S(2)}) copy-start(f32[128]{0:T(128)} %add_rsqrt_fusion.1) | copy-start | bytes 1540
  89.6 4.5 %copy-start.33 = (f32[256,768]{1,0:T(8,128)}, f32[256,768]{1,0:T(8,128)S(1)}, u32[]{:S(2)}) copy-start(f32[256,768]{1,0:T(8,128)S(1)} %convolution_add_fusion) | copy-start | bytes 2359300
  90.3 13.8 %collective-permute-start.6 = (bf16[128,768]{1,0:T(8,128)(2,1)}, bf16[128,768]{1,0:T(8,128)(2,1)}, u32[]{:S(2)}, u32[]{:S(2)}) collective-permute-start(bf16[128,768]{1,0:T(8,128)(2,1)} %fusion.42), channel_id=1, source_target_pairs={{0,1},{1,0},{2,3},{3,2},{4,5},{5,4},{6,7},{7,6},{8,9},{9,8},{10,11... | collective-permute-start | bytes 589832 | tf_op jit(solution)/shard_map/ppermute | solution.py:87
  99.9 4.2 %copy-start.34 = (f32[256,768]{1,0:T(8,128)S(1)}, f32[256,768]{1,0:T(8,128)}, u32[]{:S(2)}) copy-start(f32[256,768]{1,0:T(8,128)} %copy-done.33) | copy-start | bytes 2359300
  99.9 5.9 %copy-start.7 = (f32[256,768]{1,0:T(8,128)S(1)}, f32[256,768]{1,0:T(8,128)}, u32[]{:S(2)}) copy-start(f32[256,768]{1,0:T(8,128)} %copy-done.4) | copy-start | bytes 2359300
  99.9 5.9 %copy-start.31 = (f32[256,768]{1,0:T(8,128)S(1)}, f32[256,768]{1,0:T(8,128)}, u32[]{:S(2)}) copy-start(f32[256,768]{1,0:T(8,128)} %get-tuple-element.78) | copy-start | bytes 2359300
  99.9 5.9 %copy-start.77 = (f32[768]{0:T(1024)S(1)}, f32[768]{0:T(1024)}, u32[]{:S(2)}) copy-start(f32[768]{0:T(1024)} %param.24) | copy-start | bytes 9220
  102.5 51.6 %collective-permute-start.16 = (bf16[2,2,2,48,1536]{4,3,2,1,0:T(8,128)(2,1)}, bf16[2,2,2,48,1536]{4,3,2,1,0:T(8,128)(2,1)}, u32[]{:S(2)}, u32[]{:S(2)}) collective-permute-start(bf16[2,2,2,48,1536]{4,3,2,1,0:T(8,128)(2,1)} %dynamic-slice_bitcast_fusion.2), channel_id=1, source_target_pairs={{0,2},{2,0},{4,6},{6,4},{8,10},{10,8},{12,14},{14,12},{16,18},{18,... | collective-permute-start | bytes 3538952 | tf_op jit(solution)/shard_map/ppermute | solution.py:114
  112.2 7.2 %copy-start.58 = (bf16[6,64,256]{2,1,0:T(8,128)(2,1)}, bf16[6,64,256]{2,1,0:T(8,128)(2,1)S(1)}, u32[]{:S(2)}) copy-start(bf16[6,64,256]{2,1,0:T(8,128)(2,1)S(1)} %convolution_convert_fusion.15) | copy-start | bytes 589828
  112.5 8.5 %copy-start.59 = (bf16[6,64,256]{2,1,0:T(8,128)(2,1)}, bf16[6,64,256]{2,1,0:T(8,128)(2,1)S(1)}, u32[]{:S(2)}) copy-start(bf16[6,64,256]{2,1,0:T(8,128)(2,1)S(1)} %convolution_convert_fusion.14) | copy-start | bytes 589828
  113.2 5.0 %copy-start.15 = (f32[256,768]{1,0:T(8,128)S(1)}, f32[256,768]{1,0:T(8,128)}, u32[]{:S(2)}) copy-start(f32[256,768]{1,0:T(8,128)} %copy-done.14) | copy-start | bytes 2359300
  113.2 5.0 %copy-start.61 = (bf16[6,64,256]{2,1,0:T(8,128)(2,1)S(1)}, bf16[6,64,256]{2,1,0:T(8,128)(2,1)}, u32[]{:S(2)}) copy-start(bf16[6,64,256]{2,1,0:T(8,128)(2,1)} %copy-done.60) | copy-start | bytes 589828
  121.9 7.5 %copy-start.22 = (f32[256,768]{1,0:T(8,128)S(1)}, f32[256,768]{1,0:T(8,128)}, u32[]{:S(2)}) copy-start(f32[256,768]{1,0:T(8,128)} %convert_element_type.376) | copy-start | bytes 2359300
  121.9 7.5 %copy-start.92 = (f32[128]{0:T(128)S(1)}, f32[128]{0:T(128)}, u32[]{:S(2)}) copy-start(f32[128]{0:T(128)} %fusion.50) | copy-start | bytes 1540
  122.7 6.8 %collective-permute-start.5 = (bf16[128,768]{1,0:T(8,128)(2,1)}, bf16[128,768]{1,0:T(8,128)(2,1)}, u32[]{:S(2)}, u32[]{:S(2)}) collective-permute-start(bf16[128,768]{1,0:T(8,128)(2,1)} %fusion.41), channel_id=1, source_target_pairs={{0,1},{1,0},{2,3},{3,2},{4,5},{5,4},{6,7},{7,6},{8,9},{9,8},{10,11... | collective-permute-start | bytes 589832 | tf_op jit(solution)/shard_map/ppermute | solution.py:87
  130.7 6.3 %copy-start.37 = (bf16[768,384]{0,1:T(8,128)(2,1)S(1)}, bf16[768,384]{0,1:T(8,128)(2,1)}, u32[]{:S(2)}) copy-start(bf16[768,384]{0,1:T(8,128)(2,1)} %convolution_convert_fusion.6) | copy-start | bytes 1769476
  133.4 1.4 collective-permute-start.7
  135.5 5.3 %collective-permute-start.8 = (f32[2496]{0:T(1024)S(1)}, f32[2496]{0:T(1024)S(1)}, u32[]{:S(2)}, u32[]{:S(2)}) collective-permute-start(f32[2496]{0:T(1024)S(1)} %add.292), channel_id=1, source_target_pairs={{0,4},{2,6},{4,0},{6,2},{8,12},{10,14},{12,8},{14,10},{16,20},{18,... | collective-permute-start | bytes 29960 | tf_op jit(solution)/shard_map/ppermute | solution.py:126
  140.8 6.8 %copy-start.95 = (f32[128]{0:T(128)S(1)}, f32[128]{0:T(128)}, u32[]{:S(2)}) copy-start(f32[128]{0:T(128)} %multiply_reduce_fusion.13) | copy-start | bytes 1540
  140.8 4.1 %collective-permute-start.9 = (f32[2496]{0:T(1024)S(1)}, f32[2496]{0:T(1024)S(1)}, u32[]{:S(2)}, u32[]{:S(2)}) collective-permute-start(f32[2496]{0:T(1024)S(1)} %add.293), channel_id=1, source_target_pairs={{0,8},{2,10},{4,12},{6,14},{8,0},{10,2},{12,4},{14,6},{16,24},{18,... | collective-permute-start | bytes 29960 | tf_op jit(solution)/shard_map/ppermute | solution.py:126
  142.5 11.6 %copy-start.16 = (bf16[768,1536]{1,0:T(8,128)(2,1)S(1)}, bf16[768,1536]{1,0:T(8,128)(2,1)}, u32[]{:S(2)}) copy-start(bf16[768,1536]{1,0:T(8,128)(2,1)} %copy.95) | copy-start | bytes 7077892
  145.0 11.4 %collective-permute-start.12 = (bf16[2,2,2,48,1536]{4,3,2,1,0:T(8,128)(2,1)}, bf16[2,2,2,48,1536]{4,3,2,1,0:T(8,128)(2,1)}, u32[]{:S(2)}, u32[]{:S(2)}) collective-permute-start(bf16[2,2,2,48,1536]{4,3,2,1,0:T(8,128)(2,1)} %dynamic-slice_bitcast_fusion.3), channel_id=1, source_target_pairs={{0,2},{2,0},{4,6},{6,4},{8,10},{10,8},{12,14},{14,12},{16,18},{18,... | collective-permute-start | bytes 3538952 | tf_op jit(solution)/shard_map/ppermute | solution.py:114
  145.0 4.7 %collective-permute-start.10 = (f32[2496]{0:T(1024)S(1)}, f32[2496]{0:T(1024)S(1)}, u32[]{:S(2)}, u32[]{:S(2)}) collective-permute-start(f32[2496]{0:T(1024)S(1)} %add.294), channel_id=1, source_target_pairs={{0,16},{2,18},{4,20},{6,22},{8,24},{10,26},{12,28},{14,30},{16,0},... | collective-permute-start | bytes 29960 | tf_op jit(solution)/shard_map/ppermute | solution.py:126
  149.7 3.8 %collective-permute-start.11 = (f32[3,768]{1,0:T(4,128)S(1)}, f32[3,768]{1,0:T(4,128)S(1)}, u32[]{:S(2)}, u32[]{:S(2)}) collective-permute-start(f32[3,768]{1,0:T(4,128)S(1)} %reshape.413), channel_id=1, source_target_pairs={{0,1},{1,0},{2,3},{3,2},{4,5},{5,4},{6,7},{7,6},{8,9},{9,8},{10,11... | collective-permute-start | bytes 27656 | tf_op jit(solution)/shard_map/ppermute | solution.py:87
  155.8 16.3 %collective-permute-start.17 = (bf16[2,2,48,1536]{3,2,1,0:T(8,128)(2,1)S(1)}, bf16[2,2,48,1536]{3,2,1,0:T(8,128)(2,1)S(1)}, u32[]{:S(2)}, u32[]{:S(2)}) collective-permute-start(bf16[2,2,48,1536]{3,2,1,0:T(8,128)(2,1)S(1)} %dynamic-slice_bitcast_fusion.5), channel_id=1, source_target_pairs={{0,4},{2,6},{4,0},{6,2},{8,12},{10,14},{12,8},{14,10},{16,20},{18,... | collective-permute-start | bytes 1769480 | tf_op jit(solution)/shard_map/ppermute | solution.py:114
  158.1 26.7 %collective-permute-start.13 = (bf16[2,2,48,1536]{3,2,1,0:T(8,128)(2,1)S(1)}, bf16[2,2,48,1536]{3,2,1,0:T(8,128)(2,1)S(1)}, u32[]{:S(2)}, u32[]{:S(2)}) collective-permute-start(bf16[2,2,48,1536]{3,2,1,0:T(8,128)(2,1)S(1)} %dynamic-slice_bitcast_fusion.6), channel_id=1, source_target_pairs={{0,4},{2,6},{4,0},{6,2},{8,12},{10,14},{12,8},{14,10},{16,20},{18,... | collective-permute-start | bytes 1769480 | tf_op jit(solution)/shard_map/ppermute | solution.py:114
  172.3 8.4 %collective-permute-start.18 = (bf16[2,48,1536]{2,1,0:T(8,128)(2,1)S(1)}, bf16[2,48,1536]{2,1,0:T(8,128)(2,1)S(1)}, u32[]{:S(2)}, u32[]{:S(2)}) collective-permute-start(bf16[2,48,1536]{2,1,0:T(8,128)(2,1)S(1)} %dynamic-slice_bitcast_fusion.8), channel_id=1, source_target_pairs={{0,8},{2,10},{4,12},{6,14},{8,0},{10,2},{12,4},{14,6},{16,24},{18,... | collective-permute-start | bytes 884744 | tf_op jit(solution)/shard_map/ppermute | solution.py:114
  176.9 30.9 %collective-permute-start.21 = (bf16[2,2,48,3072]{3,2,1,0:T(8,128)(2,1)S(1)}, bf16[2,2,48,3072]{3,2,1,0:T(8,128)(2,1)S(1)}, u32[]{:S(2)}, u32[]{:S(2)}) collective-permute-start(bf16[2,2,48,3072]{3,2,1,0:T(8,128)(2,1)S(1)} %dynamic-slice_bitcast_fusion.1), channel_id=1, source_target_pairs={{0,4},{2,6},{4,0},{6,2},{8,12},{10,14},{12,8},{14,10},{16,20},{18,... | collective-permute-start | bytes 3538952 | tf_op jit(solution)/shard_map/ppermute | solution.py:114
  180.8 7.5 %collective-permute-start.19 = (bf16[48,1536]{1,0:T(8,128)(2,1)S(1)}, bf16[48,1536]{1,0:T(8,128)(2,1)S(1)}, u32[]{:S(2)}, u32[]{:S(2)}) collective-permute-start(bf16[48,1536]{1,0:T(8,128)(2,1)S(1)} %dynamic-slice_bitcast_fusion.10), channel_id=1, source_target_pairs={{0,16},{2,18},{4,20},{6,22},{8,24},{10,26},{12,28},{14,30},{16,0},... | collective-permute-start | bytes 442376 | tf_op jit(solution)/shard_map/ppermute | solution.py:114
  184.9 23.8 %collective-permute-start.14 = (bf16[2,48,1536]{2,1,0:T(8,128)(2,1)S(1)}, bf16[2,48,1536]{2,1,0:T(8,128)(2,1)S(1)}, u32[]{:S(2)}, u32[]{:S(2)}) collective-permute-start(bf16[2,48,1536]{2,1,0:T(8,128)(2,1)S(1)} %dynamic-slice_bitcast_fusion.9), channel_id=1, source_target_pairs={{0,8},{2,10},{4,12},{6,14},{8,0},{10,2},{12,4},{14,6},{16,24},{18,... | collective-permute-start | bytes 884744 | tf_op jit(solution)/shard_map/ppermute | solution.py:114
  208.3 16.3 %collective-permute-start.22 = (bf16[2,48,3072]{2,1,0:T(8,128)(2,1)S(1)}, bf16[2,48,3072]{2,1,0:T(8,128)(2,1)S(1)}, u32[]{:S(2)}, u32[]{:S(2)}) collective-permute-start(bf16[2,48,3072]{2,1,0:T(8,128)(2,1)S(1)} %dynamic-slice_bitcast_fusion.4), channel_id=1, source_target_pairs={{0,8},{2,10},{4,12},{6,14},{8,0},{10,2},{12,4},{14,6},{16,24},{18,... | collective-permute-start | bytes 1769480 | tf_op jit(solution)/shard_map/ppermute | solution.py:114
  208.9 17.0 %collective-permute-start.15 = (bf16[48,1536]{1,0:T(8,128)(2,1)S(1)}, bf16[48,1536]{1,0:T(8,128)(2,1)S(1)}, u32[]{:S(2)}, u32[]{:S(2)}) collective-permute-start(bf16[48,1536]{1,0:T(8,128)(2,1)S(1)} %dynamic-slice_bitcast_fusion.11), channel_id=1, source_target_pairs={{0,16},{2,18},{4,20},{6,22},{8,24},{10,26},{12,28},{14,30},{16,0},... | collective-permute-start | bytes 442376 | tf_op jit(solution)/shard_map/ppermute | solution.py:114
  224.8 14.5 %collective-permute-start.23 = (bf16[48,3072]{1,0:T(8,128)(2,1)S(1)}, bf16[48,3072]{1,0:T(8,128)(2,1)S(1)}, u32[]{:S(2)}, u32[]{:S(2)}) collective-permute-start(bf16[48,3072]{1,0:T(8,128)(2,1)S(1)} %dynamic-slice_bitcast_fusion.7), channel_id=1, source_target_pairs={{0,16},{2,18},{4,20},{6,22},{8,24},{10,26},{12,28},{14,30},{16,0},... | collective-permute-start | bytes 884744 | tf_op jit(solution)/shard_map/ppermute | solution.py:114
  225.8 14.3 %copy-start.1 = (bf16[768,1024]{1,0:T(8,128)(2,1)S(1)}, bf16[768,1024]{1,0:T(8,128)(2,1)}, u32[]{:S(2)}) copy-start(bf16[768,1024]{1,0:T(8,128)(2,1)} %param.35) | copy-start | bytes 4718596
  (57 other events, 85.6 us)

commit v2 on v1

v2 whole, which is shorter than its diff:
```python
import functools

import jax
import jax.numpy as jnp
from jax import lax
from jax.experimental import pallas as pl
from jax.experimental.pallas import tpu as pltpu
from jax.sharding import PartitionSpec as P


HD = 64
LEN = 256
LANES = 128
PIECE = 256


epsilon = 1e-06
masked = -1e30
bend = 0.044715
slope = 0.7978845608028654

f32 = jnp.float32
bf16 = jnp.bfloat16


def dot(left, right):
    return jnp.dot(left, right, preferred_element_type=f32)


def dot_back(left, weight):
    return lax.dot_general(left, weight, (((1,), (1,)), ((), ())), preferred_element_type=f32)


def dot_outer(left, right):
    return lax.dot_general(left, right, (((0,), (0,)), ((), ())), preferred_element_type=f32)


def rms(hidden, gain):
    scale = lax.rsqrt(jnp.mean(hidden * hidden, axis=-1, keepdims=True) + epsilon)
    return hidden * scale * gain


def rms_back(hidden, gain, grad):
    scale = lax.rsqrt(jnp.mean(hidden * hidden, axis=-1, keepdims=True) + epsilon)
    unit = hidden * scale
    pulled = grad * gain
    along = jnp.mean(pulled * unit, axis=-1, keepdims=True)
    return scale * (pulled - unit * along), grad * unit


def pair_mask(rows, side):
    lane = lax.broadcasted_iota(jnp.int32, (rows, LANES), 1)
    return (lane >= HD) == (side == 1)


def keep_side(rows, side):
    return jnp.where(pair_mask(rows.shape[0], side), rows, jnp.zeros_like(rows))


def softmax(scores):
    top = jnp.max(scores, axis=-1, keepdims=True)
    weights = jnp.exp(scores - top)
    return weights * (1.0 / jnp.sum(weights, axis=-1, keepdims=True))


def heads_forward(query, keys, values, extra_of, probs_out, mixed_out):
    for pair in range(query.shape[1] // LANES):
        lanes = slice(pair * LANES, (pair + 1) * LANES)
        probs, sides = [], []
        for side in range(2):
            scores = dot_back(keep_side(query[:, lanes], side), keys[:, lanes])
            head_probs = softmax(extra_of(scores, 2 * pair + side))
            probs_out[2 * pair + side] = head_probs
            probs.append(head_probs.astype(bf16))
            sides.append(keep_side(values[:, lanes], side))
        mixed = dot(jnp.concatenate(probs, axis=1), jnp.concatenate(sides, axis=0))
        mixed_out[:, lanes] = mixed.astype(bf16)


def heads_backward(query, keys, values, probs_in, grad_mixed, outs, dscore_out):
    dquery_out, dkeys_out, dvalues_out = outs
    for pair in range(query.shape[1] // LANES):
        lanes = slice(pair * LANES, (pair + 1) * LANES)
        scores_low, key_sides, query_sides, probs_low, grad_sides = [], [], [], [], []
        for side in range(2):
            probs = probs_in[2 * pair + side]
            grad_side = keep_side(grad_mixed[:, lanes], side)
            dprob = dot_back(grad_side, values[:, lanes])
            dscore = probs * (dprob - jnp.sum(probs * dprob, axis=-1, keepdims=True))
            if dscore_out is not None:
                dscore_out[2 * pair + side] = dscore
            scores_low.append(dscore.astype(bf16))
            probs_low.append(probs.astype(bf16))
            key_sides.append(keep_side(keys[:, lanes], side))
            query_sides.append(keep_side(query[:, lanes], side))
            grad_sides.append(grad_side)
        dquery = dot(jnp.concatenate(scores_low, axis=1), jnp.concatenate(key_sides, axis=0))
        dquery_out[:, lanes] = dquery.astype(bf16)
        dkeys = dot_outer(
            jnp.concatenate(scores_low, axis=0), jnp.concatenate(query_sides, axis=0)
        )
        dkeys_out[:, lanes] = dkeys.astype(bf16)
        dvalues = dot_outer(
            jnp.concatenate(probs_low, axis=0), jnp.concatenate(grad_sides, axis=0)
        )
        dvalues_out[:, lanes] = dvalues.astype(bf16)


def own_part(terms):
    share = terms.shape[0] // 2
    row = lax.broadcasted_iota(jnp.int32, terms.shape, 0)
    mine = (row >= share) == (lax.axis_index("tensor") == 1)
    return jnp.sum(jnp.where(mine, terms, 0.0), axis=0, keepdims=True)


def own_rows_of(ref, other=False):
    share = ref.shape[0] // 2
    index = lax.axis_index("tensor")
    index = 1 - index if other else index
    return ref[pl.ds(pl.multiple_of(index * share, share), share), :]


def self_forward(
    inputs, gain, sq, sk, sv, so, buckets, table,
    normed_out, q_out, k_out, v_out, probs_out, mixed_out, kept_out, sent_out,
):
    normed = rms(inputs[...].astype(f32), gain[...]).astype(bf16)
    normed_out[...] = normed
    q_out[...] = dot(normed, sq[...]).astype(bf16)
    k_out[...] = dot(normed, sk[...]).astype(bf16)
    v_out[...] = dot(normed, sv[...]).astype(bf16)
    count = table.shape[1]
    row = lax.broadcasted_iota(jnp.int32, (count, LANES), 0)
    lane = lax.broadcasted_iota(jnp.int32, (count, LANES), 1)
    by_lane = jnp.dot(
        table[...],
        (row == lane).astype(f32),
        preferred_element_type=f32,
        precision=lax.Precision.HIGHEST,
    )
    length = inputs.shape[0]
    causal = lax.broadcasted_iota(jnp.int32, (length, length), 1) <= lax.broadcasted_iota(
        jnp.int32, (length, length), 0
    )

    def extra_of(scores, head):
        values = jnp.broadcast_to(by_lane[head : head + 1, :], (length, LANES))
        bias = jnp.concatenate(
            [
                jnp.take_along_axis(
                    values,
                    buckets[:, at : at + LANES],
                    axis=1,
                    mode="promise_in_bounds",
                )
                for at in range(0, length, LANES)
            ],
            axis=1,
        )
        return jnp.where(causal, scores + bias, masked)

    heads_forward(q_out, k_out, v_out, extra_of, probs_out, mixed_out)
    part = dot(mixed_out[...], so[...])
    kept_out[...] = part
    sent_out[...] = part.astype(bf16)


def cross_keys(encoded, ck, cv, k_out, v_out):
    k_out[...] = dot(encoded[...], ck[...]).astype(bf16)
    v_out[...] = dot(encoded[...], cv[...]).astype(bf16)


def cross_forward(
    inputs, kept, got, gain, cq, keys, values, co,
    first_out, normed_out, q_out, probs_out, mixed_out, kept_out, sent_out,
):
    first = inputs[...].astype(f32) + (kept[...] + got[...].astype(f32))
    first_out[...] = first
    normed = rms(first, gain[...]).astype(bf16)
    normed_out[...] = normed
    q_out[...] = dot(normed, cq[...]).astype(bf16)
    heads_forward(q_out, keys, values, lambda scores, head: scores, probs_out, mixed_out)
    part = dot(mixed_out[...], co[...])
    kept_out[...] = part
    sent_out[...] = part.astype(bf16)


def hidden_back(cotangent, fd, dhidden_out):
    dhidden_out[...] = dot_back(cotangent[...], fd[...])


def ffn_both(
    first, kept, got, gain, fg, fu, dhidden,
    second_out, normed_out, hidden_out, dgate_out, dup_out, kept_out, sent_out,
):
    second = first[...] + (kept[...] + got[...].astype(f32))
    second_out[...] = second
    normed = rms(second, gain[...]).astype(bf16)
    normed_out[...] = normed
    total = jnp.zeros(second.shape, f32)
    for at in range(0, fg.shape[1], PIECE):
        units = slice(at, at + PIECE)
        gate = dot(normed, fg[:, units])
        up = dot(normed, fu[:, units])
        square = gate * gate
        bent = jnp.tanh(slope * (gate + bend * (square * gate)))
        half = 0.5 * (1.0 + bent)
        gelu = gate * half
        hidden_out[:, units] = (gelu * up).astype(bf16)
        rise = half + 0.5 * gate * (1.0 - bent * bent) * (slope * (1.0 + 3.0 * bend * square))
        grad = dhidden[:, units]
        dgate = (grad * up * rise).astype(bf16)
        dup = (grad * gelu).astype(bf16)
        dgate_out[:, units] = dgate
        dup_out[:, units] = dup
        total = total + (dot_back(dgate, fg[:, units]) + dot_back(dup, fu[:, units]))
    kept_out[...] = total
    sent_out[...] = total.astype(bf16)


def ffn_output(hidden, fd, second, kept_out, sent_out, total):
    total[...] = dot(hidden[...], fd[...])
    kept_out[...] = own_rows_of(second) + own_rows_of(total)
    sent_out[...] = own_rows_of(total, True).astype(bf16)


def cross_backward(
    second, cotangent, kept, got, gain, co, cq, query, keys, values, probs,
    dsecond_out, low_out, dq_out, dk_out, dv_out, kept_out, sent_out, gain_out,
):
    back, terms = rms_back(second[...], gain[...], kept[...] + got[...].astype(f32))
    gain_out[...] = own_part(terms)
    dsecond = cotangent[...].astype(f32) + back
    dsecond_out[...] = dsecond
    low = dsecond.astype(bf16)
    low_out[...] = low
    grad_mixed = dot_back(low, co[...]).astype(bf16)
    heads_backward(query, keys, values, probs, grad_mixed, (dq_out, dk_out, dv_out), None)
    part = dot_back(dq_out[...], cq[...])
    kept_out[...] = part
    sent_out[...] = part.astype(bf16)


def encoded_back(dk, dv, ck, cv, kept_out, sent_out, total):
    total[...] = dot_back(dk[...], ck[...]) + dot_back(dv[...], cv[...])
    kept_out[...] = own_rows_of(total)
    sent_out[...] = own_rows_of(total, True).astype(bf16)


def self_backward(
    first, dsecond, kept, got, gain, so, sq, sk, sv, query, keys, values, probs,
    dfirst_out, low_out, dq_out, dk_out, dv_out, dscore_out, kept_out, sent_out, gain_out, total,
):
    back, terms = rms_back(first[...], gain[...], kept[...] + got[...].astype(f32))
    gain_out[...] = own_part(terms)
    dfirst = dsecond[...] + back
    total[...] = dfirst
    dfirst_out[...] = own_rows_of(total)
    low = dfirst.astype(bf16)
    low_out[...] = low
    grad_mixed = dot_back(low, so[...]).astype(bf16)
    heads_backward(query, keys, values, probs, grad_mixed, (dq_out, dk_out, dv_out), dscore_out)
    total[...] = (
        dot_back(dq_out[...], sq[...]) + dot_back(dk_out[...], sk[...])
    ) + dot_back(dv_out[...], sv[...])
    kept_out[...] = own_rows_of(total)
    sent_out[...] = own_rows_of(total, True).astype(bf16)


def last_back(inputs, dfirst, kept, got, gain, grad_out, gain_out):
    own = own_rows_of(inputs).astype(f32)
    back, terms = rms_back(own, gain[...], kept[...] + got[...].astype(f32))
    gain_out[...] = jnp.sum(terms, axis=0, keepdims=True)
    grad_out[...] = dfirst[...] + back


def weight_grads(places, block, *refs):
    inputs, (kept_out, sent_out, product) = refs[:-3], refs[-3:]
    side = lax.axis_index("dp") & 1
    column = 0
    turned = {}
    for left, right in places:
        if left not in turned:
            turned[left] = inputs[left][...].T
        width = inputs[right].shape[1]
        for at in range(0, width, PIECE):
            span = min(PIECE, width - at)
            product[:, :span] = dot(turned[left], inputs[right][:, at : at + span])
            columns = slice(column, column + span)
            for pair in range(product.shape[0] // (2 * block)):
                rows = slice(pair * block, (pair + 1) * block)
                kept_at = pl.multiple_of((2 * pair + side) * block, 16)
                sent_at = pl.multiple_of((2 * pair + 1 - side) * block, 16)
                kept_out[rows, columns] = product[pl.ds(kept_at, block), :span].astype(bf16)
                sent_out[rows, columns] = product[pl.ds(sent_at, block), :span].astype(bf16)
            column += span


def halve(block, bit, kept, got, kept_out, sent_out):
    side = (lax.axis_index("dp") >> bit) & 1
    for pair in range(kept.shape[0] // (2 * block)):
        rows = slice(pair * block, (pair + 1) * block)
        for place, out in ((side, kept_out), (1 - side, sent_out)):
            at = pl.ds(pl.multiple_of((2 * pair + place) * block, 16), block)
            out[rows, :] = (kept[at, :].astype(f32) + got[at, :].astype(f32)).astype(bf16)


def finish(kept, got, *outs):
    column = 0
    for out in outs:
        columns = slice(column, column + out.shape[1])
        out[...] = kept[:, columns].astype(f32) + got[:, columns].astype(f32)
        column += out.shape[1]


def table_grad(dscore, buckets, out, lines):
    count = out.shape[1]

    def add_bucket(bucket, carry):
        hit = buckets[...] == bucket
        for head in range(dscore.shape[0]):
            chosen = jnp.where(hit, dscore[head], 0.0)
            lines[head, pl.ds(bucket, 1), :] = jnp.sum(chosen, axis=0, keepdims=True)
        return carry

    lax.fori_loop(0, count, add_bucket, 0)
    out[...] = jnp.sum(lines[...], axis=-1)


def shape(dims, kind):
    return jax.ShapeDtypeStruct(dims, kind)


def call(kernel, outs, args, flops, scratch=()):
    moved = sum(item.size * item.dtype.itemsize for item in (*outs, *args))
    return pl.pallas_call(
        kernel,
        out_shape=tuple(outs),
        scratch_shapes=list(scratch),
        compiler_params=pltpu.CompilerParams(vmem_limit_bytes=24 << 20),
        cost_estimate=pl.CostEstimate(flops=flops, bytes_accessed=moved, transcendentals=0),
    )(*args)


def flips(size, bit):
    return [(index, index ^ bit) for index in range(size)]


def swap_tensor(value):
    return lax.ppermute(value, "tensor", flips(lax.axis_size("tensor"), 1))


def grads_of(arrays, places, block):
    rows = arrays[places[0][0]].shape[1]
    width = sum(arrays[right].shape[1] for _, right in places)
    if block % 16 == 0:
        flops = 2 * LEN * rows * width
        half = shape((rows // 2, width), bf16)
        return call(
            functools.partial(weight_grads, places, block),
            (half, half),
            arrays,
            flops,
            [pltpu.VMEM((rows, PIECE), f32)],
        )
    parts = [dot_outer(arrays[left], arrays[right]).astype(bf16) for left, right in places]
    whole = jnp.concatenate(parts, axis=1).reshape(-1, 2, block, width)
    side = lax.axis_index("dp") & 1
    kept = lax.dynamic_index_in_dim(whole, side, 1, keepdims=False)
    sent = lax.dynamic_index_in_dim(whole, 1 - side, 1, keepdims=False)
    return kept.reshape(-1, width), sent.reshape(-1, width)


def scatter_dp(kept, sent, widths):
    size = lax.axis_size("dp")
    bits = size.bit_length() - 1
    index = lax.axis_index("dp")
    columns = kept.shape[1]
    block = kept.shape[0] * 2 // size
    for bit in range(bits):
        received = lax.ppermute(sent, "dp", flips(size, 1 << bit))
        if bit == bits - 1:
            outs = [shape((block, width), f32) for width in widths]
            return call(finish, outs, (kept, received), 0)
        if block % 16 == 0:
            half = shape((kept.shape[0] // 2, columns), bf16)
            kept, sent = call(
                functools.partial(halve, block, bit + 1), (half, half), (kept, received), 0
            )
        else:
            held = (kept.astype(f32) + received.astype(f32)).astype(bf16)
            held = held.reshape(-1, 2, block, columns)
            side = (index >> (bit + 1)) & 1
            kept = lax.dynamic_index_in_dim(held, side, 1, keepdims=False)
            sent = lax.dynamic_index_in_dim(held, 1 - side, 1, keepdims=False)
            kept, sent = kept.reshape(-1, columns), sent.reshape(-1, columns)


def sum_small(gains, table):
    size = lax.axis_size("dp")
    packed = jnp.concatenate([gains.reshape(-1), table.reshape(-1)])
    bit = 1
    while bit < size:
        packed = packed + lax.ppermute(packed, "dp", flips(size, bit))
        bit *= 2
    gains = packed[: gains.size].reshape(gains.shape)
    gains = gains + swap_tensor(gains)
    return gains, packed[gains.size :].reshape(table.shape)


def body(
    inputs,
    encoded,
    cotangent,
    buckets,
    gain_self,
    gain_cross,
    gain_ffn,
    bias_table,
    self_query,
    self_attention_key,
    self_value,
    self_out,
    cross_query,
    cross_key,
    cross_value,
    cross_out,
    ffn_gate,
    ffn_up,
    ffn_down,
):
    rows, width = inputs.shape
    assert rows == LEN and encoded.shape[0] == LEN and lax.axis_size("tensor") == 2
    heads_width = self_query.shape[1]
    heads = heads_width // HD
    units = ffn_gate.shape[1]
    assert heads_width % LANES == 0 and units % PIECE == 0
    block = width // lax.axis_size("dp")
    share = rows // 2
    gain_self = gain_self.reshape(1, width)
    gain_cross = gain_cross.reshape(1, width)
    gain_ffn = gain_ffn.reshape(1, width)
    full32, full16 = shape((rows, width), f32), shape((rows, width), bf16)
    half32, half16 = shape((share, width), f32), shape((share, width), bf16)
    mix16 = shape((rows, heads_width), bf16)
    hid16 = shape((rows, units), bf16)
    probs32 = shape((heads, rows, rows), f32)
    line = shape((1, width), f32)
    scratch = [pltpu.VMEM((rows, width), f32)]
    one = 2 * rows * width * heads_width
    wide = 2 * rows * width * units

    normed1, q1, k1, v1, probs1, mixed1, kept1, sent1 = call(
        self_forward,
        (full16, mix16, mix16, mix16, probs32, mix16, full32, full16),
        (inputs, gain_self, self_query, self_attention_key, self_value, self_out, buckets, bias_table.T),
        6 * one,
    )
    got1 = swap_tensor(sent1)
    k2, v2 = call(cross_keys, (mix16, mix16), (encoded, cross_key, cross_value), 2 * one)
    first, normed2, q2, probs2, mixed2, kept2, sent2 = call(
        cross_forward,
        (full32, full16, mix16, probs32, mix16, full32, full16),
        (inputs, kept1, got1, gain_cross, cross_query, k2, v2, cross_out),
        4 * one,
    )
    got2 = swap_tensor(sent2)
    (dhidden,) = call(hidden_back, (shape((rows, units), f32),), (cotangent, ffn_down), wide)
    second, normed3, hidden, dgate, dup, kept4, sent4 = call(
        ffn_both,
        (full32, full16, hid16, hid16, hid16, full32, full16),
        (first, kept2, got2, gain_ffn, ffn_gate, ffn_up, dhidden),
        4 * wide,
    )
    got4 = swap_tensor(sent4)
    ffn_kept, ffn_sent = grads_of(
        (cotangent, hidden, normed3, dgate, dup), ((0, 1), (2, 3), (2, 4)), block
    )
    kept3, sent3 = call(ffn_output, (half32, half16), (hidden, ffn_down, second), wide, scratch)
    dsecond, low2, dq2, dk2, dv2, kept5, sent5, gain_two = call(
        cross_backward,
        (full32, full16, mix16, mix16, mix16, full32, full16, line),
        (second, cotangent, kept4, got4, gain_ffn, cross_out, cross_query, q2, k2, v2, probs2),
        5 * one,
    )
    got3 = swap_tensor(sent3)
    output = (kept3 + got3.astype(f32)).astype(bf16)
    got5 = swap_tensor(sent5)
    cross_kept, cross_sent = grads_of(
        (low2, mixed2, normed2, dq2, encoded, dk2, dv2), ((0, 1), (2, 3), (4, 5), (4, 6)), block
    )
    kept7, sent7 = call(
        encoded_back, (half32, half16), (dk2, dv2, cross_key, cross_value), 2 * one, scratch
    )
    dfirst, low1, dq1, dk1, dv1, dscore1, kept6, sent6, gain_one = call(
        self_backward,
        (half32, full16, mix16, mix16, mix16, probs32, half32, half16, line),
        (
            first, dsecond, kept5, got5, gain_cross, self_out, self_query,
            self_attention_key, self_value, q1, k1, v1, probs1,
        ),
        7 * one,
        scratch,
    )
    got7 = swap_tensor(sent7)
    grad_encoded = kept7 + got7.astype(f32)
    self_kept, self_sent = grads_of(
        (low1, mixed1, normed1, dq1, dk1, dv1), ((0, 1), (2, 3), (2, 4), (2, 5)), block
    )
    got6 = swap_tensor(sent6)
    input_grad, gain_zero = call(
        last_back, (half32, line), (inputs, dfirst, kept6, got6, gain_self), 0
    )
    table_hits = call(
        table_grad,
        (shape((heads, bias_table.shape[0]), f32),),
        (dscore1, buckets),
        0,
        [pltpu.VMEM((heads, bias_table.shape[0], rows), f32)],
    )[0]
    wide_parts = scatter_dp(ffn_kept, ffn_sent, (units,) * 3)
    cross_parts = scatter_dp(cross_kept, cross_sent, (heads_width,) * 4)
    self_parts = scatter_dp(self_kept, self_sent, (heads_width,) * 4)
    gains, table_total = sum_small(
        jnp.concatenate([gain_zero, gain_one, gain_two], axis=0), table_hits
    )
    return (
        output,
        input_grad,
        grad_encoded,
        gains[0],
        gains[1],
        gains[2],
        table_total.T,
        self_parts[1],
        self_parts[2],
        self_parts[3],
        self_parts[0].T,
        cross_parts[1],
        cross_parts[2],
        cross_parts[3],
        cross_parts[0].T,
        wide_parts[1],
        wide_parts[2],
        wide_parts[0].T,
    )


def solution(mesh):
    in_specs = (
        P("dp", None),
        P("dp", None),
        P("dp", None),
        P(),
        P(),
        P(),
        P(),
        P(None, "tensor"),
        P(None, "tensor"),
        P(None, "tensor"),
        P(None, "tensor"),
        P("tensor", None),
        P(None, "tensor"),
        P(None, "tensor"),
        P(None, "tensor"),
        P("tensor", None),
        P(None, "tensor"),
        P(None, "tensor"),
        P("tensor", None),
    )
    out_specs = (
        P(("dp", "tensor"), None),
        P(("dp", "tensor"), None),
        P(("dp", "tensor"), None),
        P(),
        P(),
        P(),
        P(None, "tensor"),
        P("dp", "tensor"),
        P("dp", "tensor"),
        P("dp", "tensor"),
        P("tensor", "dp"),
        P("dp", "tensor"),
        P("dp", "tensor"),
        P("dp", "tensor"),
        P("tensor", "dp"),
        P("dp", "tensor"),
        P("dp", "tensor"),
        P("tensor", "dp"),
    )
    return jax.shard_map(body, mesh=mesh, in_specs=in_specs, out_specs=out_specs, check_vma=False)
```

time: 241 us -> 180 us (0.75)
  Pallas kernels: 0 us -> 49 us
  matrix products: 44.9 us -> 0 us
  local copies, waits for them, and re-layouts: 54.4 us -> 19.1 us
  other arithmetic: 32.8 us -> 2.45 us
  starting transfers between devices: 25.1 us -> 30.7 us
  waiting for transfers between devices: 81.1 us -> 77.1 us
    pallas_call x0 -> x26, Pallas kernels: none -> 49 us  [call(): pl.pallas_call(kernel, out_shape=tuple(outs), scratch_shapes=list(scratch...]
    dot_general x47 -> x0, matrix products: 44.9 us -> none  [the longest x11 10.7 us: matmul(): return jnp.dot(left, right, preferred_element_type=jnp.float32)]
    ppermute x12, waiting for transfers between devices: 64.3 us -> 39.1 us  [scatter_dp(): received = lax.ppermute(sent, 'dp', flips(size, 1 << bit))]
    ppermute x8, waiting for transfers between devices: 14.7 us -> 33.4 us  [swap_tensor(): return lax.ppermute(value, 'tensor', flips(lax.axis_size('tensor'), 1))]
    concatenate x3 -> x0, local copies, waits for them, and re-layouts: 13.4 us -> none  [the longest x1 6.63 us: body(): jnp.concatenate([outer_product(cotangent, hidden).astype(jnp.bfloat16), o...]
    convert_element_type x11 -> x0, local copies, waits for them, and re-layouts: 12.6 us -> none  [the longest x3 2.11 us: scatter_tensor(): return kept + swap_tensor(sent.astype(jnp.bfloat16)).astype(jnp.float32)]
    reduce_sum x13 -> x0, other arithmetic: 10.5 us -> none  [the longest x5 5.5 us: rms_apply(): return hidden * scale * gain]
    squeeze x12 -> x0, local copies, waits for them, and re-layouts: 8.72 us -> none  [scatter_dp(): sent = lax.dynamic_index_in_dim(held, 1 - side, axis, keepdims=False)]
  transfers between devices with their start and end apart: 24 -> 24, of which waited for: 12 -> 14; matrix products, arithmetic and copies ran while one was open for 38% -> 3% of each run, Pallas kernels for 0% -> 20%
where the time goes in v2:
time: 180 us; the launch traced here: 179 us
  waiting for transfers between devices  77.1 us (43%)
  Pallas kernels  49 us (27%)
  starting transfers between devices  30.7 us (17%)
  local copies, waits for them, and re-layouts  19.1 us (11%)
  other arithmetic  2.45 us (1%)
    pallas_call x26, Pallas kernels, call(): pl.pallas_call(kernel, out_shape=tuple(outs), scratch_shapes=list(scratch...  49 us
    ppermute x12, waiting for transfers between devices, scatter_dp(): received = lax.ppermute(sent, 'dp', flips(size, 1 << bit))  39.1 us
    ppermute x8, waiting for transfers between devices, swap_tensor(): return lax.ppermute(value, 'tensor', flips(lax.axis_size('tensor'), 1))  33.4 us
    unnamed x103, local copies, waits for them, and re-layouts  16.4 us
    ppermute x12, starting transfers between devices, scatter_dp(): received = lax.ppermute(sent, 'dp', flips(size, 1 << bit))  14 us
    ppermute x8, starting transfers between devices, swap_tensor(): return lax.ppermute(value, 'tensor', flips(lax.axis_size('tensor'), 1))  12 us
    ppermute x4, starting transfers between devices, sum_small(): packed = packed + lax.ppermute(packed, 'dp', flips(size, bit))  4.67 us
    ppermute x4, waiting for transfers between devices, sum_small(): packed = packed + lax.ppermute(packed, 'dp', flips(size, bit))  4.64 us
  transfers between devices with their start and end apart: 24, of which 14 were waited for; matrix products, arithmetic and copies ran while one was open for 3% of the time, Pallas kernels for 20%

profile of v2, /device:TPU:0, one launch (start us, length us, event | category | flops | bytes accessed | tf_op | source)
XLA Modules:
  0.0 179.3 jit_solution(15205519825875123493)
XLA Ops:
  1.3 1.0 copy-done.7
  2.3 1.1 copy-done.15
  3.4 1.1 copy-done.17
  4.5 1.1 copy-done.19
  5.5 1.1 copy-done.21
  6.6 0.9 copy-done.40
  8.2 3.3 %shard_map.322 = (bf16[256,768]{1,0:T(8,128)(2,1)S(1)}, bf16[256,384]{1,0:T(8,128)(2,1)S(1)}, bf16[256,384]{1,0:T(8,128)(2,1)S(1)}, bf16[256,384]{1,0:T(8,128)(2...) custom-call(bf16[256,768]{1,0:T(8,128)(2,1)S(1)} %copy-done.7, ...), custom_call_target="tpu_custom_call" | custom-call | flops 905969664 | bytes 6950656 | tf_op jit(solution)/shard_map/pallas_call | solution.py:336
  11.6 3.1 %collective-permute-start = (bf16[256,768]{1,0:T(8,128)(2,1)S(1)}, bf16[256,768]{1,0:T(8,128)(2,1)S(1)}, u32[]{:S(2)}, u32[]{:S(2)}) collective-permute-start(bf16[256,768]{1,0:T(8,128)(2,1)S(1)} %get-tuple-element.101), channel_id=1, source_target_pairs={{0,1},{1,0},{2,3},{3,2},{4,5},{5,4},{6,7},{7,6},{8,9},{9,8},{10,11... | collective-permute-start | bytes 1179656 | tf_op jit(solution)/shard_map/ppermute | solution.py:350
  15.3 8.5 %collective-permute-done.got = bf16[256,768]{1,0:T(8,128)(2,1)S(1)} collective-permute-done((bf16[256,768]{1,0:T(8,128)(2,1)S(1)}, bf16[256,768]{1,0:T(8,128)(2,1)S(1)}, u32[]{:S(2)}, u32[]{:S(2)}) %collective-permute-start) | collective-permute-done | bytes 393248 | tf_op jit(solution)/shard_map/ppermute | solution.py:350
  23.8 2.1 %shard_map.324 = (f32[256,768]{1,0:T(8,128)S(1)}, bf16[256,768]{1,0:T(8,128)(2,1)S(1)}, bf16[256,384]{1,0:T(8,128)(2,1)S(1)}, f32[6,256,256]{2,1,0:T(8,128)S(1)}...) custom-call(bf16[256,768]{1,0:T(8,128)(2,1)S(1)} %copy-done.8, ...), custom_call_target="tpu_custom_call" | custom-call | flops 603979776 | bytes 7474176 | tf_op jit(solution)/shard_map/pallas_call | solution.py:336
  25.9 1.8 %collective-permute-start.1 = (bf16[256,768]{1,0:T(8,128)(2,1)S(1)}, bf16[256,768]{1,0:T(8,128)(2,1)S(1)}, u32[]{:S(2)}, u32[]{:S(2)}) collective-permute-start(bf16[256,768]{1,0:T(8,128)(2,1)S(1)} %get-tuple-element.106), channel_id=1, source_target_pairs={{0,1},{1,0},{2,3},{3,2},{4,5},{5,4},{6,7},{7,6},{8,9},{9,8},{10,11... | collective-permute-start | bytes 1179656 | tf_op jit(solution)/shard_map/ppermute | solution.py:350
  28.4 7.9 %collective-permute-done.1.got = bf16[256,768]{1,0:T(8,128)(2,1)S(1)} collective-permute-done((bf16[256,768]{1,0:T(8,128)(2,1)S(1)}, bf16[256,768]{1,0:T(8,128)(2,1)S(1)}, u32[]{:S(2)}, u32[]{:S(2)}) %collective-permute-start.1) | collective-permute-done | bytes 393248 | tf_op jit(solution)/shard_map/ppermute | solution.py:350
  36.3 2.7 %shard_map.326 = (f32[256,768]{1,0:T(8,128)S(1)}, bf16[256,768]{1,0:T(8,128)(2,1)S(1)}, bf16[256,1024]{1,0:T(8,128)(2,1)S(1)}, bf16[256,1024]{1,0:T(8,128)(2,1)S...) custom-call(f32[256,768]{1,0:T(8,128)S(1)} %get-tuple-element.104.first, ...), custom_call_target="tpu_custom_call" | custom-call | flops 1610612736 | bytes 10095616 | tf_op jit(solution)/shard_map/pallas_call | solution.py:336
  39.0 3.5 %shard_map.343 = (bf16[384,3072]{1,0:T(8,128)(2,1)S(1)}, bf16[384,3072]{1,0:T(8,128)(2,1)S(1)}) custom-call(bf16[256,768]{1,0:T(8,128)(2,1)S(1)} %copy-done.12, bf16[256,1024]{1,0:T(8,128)(2,1)S(1)} %get-tuple-element.107.hidden.refs_1_, bf16[256,768]{1,0:T(8,128)(2,1)S(1)} %get-tuple-element.168.refs_2_, bf16[256,1024]{1,0:T(8,128)(2,1)S(1)} %get-tuple-element.169.refs_3_, ...), custom_call_target="tpu_custom_call" | custom-call | flops 1207959552 | bytes 7077888 | tf_op jit(solution)/shard_map/pallas_call | solution.py:336
  42.6 1.5 collective-permute-start.3
  44.1 10.0 %collective-permute-done.3.got = bf16[256,768]{1,0:T(8,128)(2,1)S(1)} collective-permute-done((bf16[256,768]{1,0:T(8,128)(2,1)S(1)}, bf16[256,768]{1,0:T(8,128)(2,1)S(1)}, u32[]{:S(2)}, u32[]{:S(2)}) %collective-permute-start.3) | collective-permute-done | bytes 393248 | tf_op jit(solution)/shard_map/ppermute | solution.py:350
  54.1 2.9 %shard_map.328 = (f32[256,768]{1,0:T(8,128)S(1)}, bf16[256,768]{1,0:T(8,128)(2,1)S(1)}, bf16[256,384]{1,0:T(8,128)(2,1)S(1)}, bf16[256,384]{1,0:T(8,128)(2,1)S(1...) custom-call(f32[256,768]{1,0:T(8,128)S(1)} %get-tuple-element.108.se, ...), custom_call_target="tpu_custom_call" | custom-call | flops 754974720 | bytes 8656896 | tf_op jit(solution)/shard_map/pallas_call | solution.py:336
  57.0 1.5 collective-permute-start.4
  58.6 2.1 %shard_map.338 = (bf16[384,1536]{1,0:T(8,128)(2,1)S(1)}, bf16[384,1536]{1,0:T(8,128)(2,1)S(1)}) custom-call(bf16[256,768]{1,0:T(8,128)(2,1)S(1)} %get-tuple-element.152.refs_0_, bf16[256,384]{1,0:T(8,128)(2,1)S(1)} %get-tuple-element.153.refs_1_, bf16[256,768]{1,0:T(8,128)(2,1)S(1)} %get-tuple-element.154.refs_2_, ...), custom_call_target="tpu_custom_call" | custom-call | flops 603979776 | bytes 4325376 | tf_op jit(solution)/shard_map/pallas_call | solution.py:336
  60.7 7.0 %collective-permute-done.4.got = bf16[256,768]{1,0:T(8,128)(2,1)S(1)} collective-permute-done((bf16[256,768]{1,0:T(8,128)(2,1)S(1)}, bf16[256,768]{1,0:T(8,128)(2,1)S(1)}, u32[]{:S(2)}, u32[]{:S(2)}) %collective-permute-start.4) | collective-permute-done | bytes 393248 | tf_op jit(solution)/shard_map/ppermute | solution.py:350
  67.7 4.3 %shard_map.329 = (f32[128,768]{1,0:T(8,128)S(1)}, bf16[256,768]{1,0:T(8,128)(2,1)S(1)}, bf16[256,384]{1,0:T(8,128)(2,1)S(1)}, bf16[256,384]{1,0:T(8,128)(2,1)S(1...) custom-call(f32[256,768]{1,0:T(8,128)S(1)} %get-tuple-element.104.fi, ...), custom_call_target="tpu_custom_call" | custom-call | flops 1056964608 | bytes 10819584 | tf_op jit(solution)/shard_map/pallas_call | solution.py:336
  72.0 2.0 %shard_map.333 = (bf16[384,1536]{1,0:T(8,128)(2,1)S(1)}, bf16[384,1536]{1,0:T(8,128)(2,1)S(1)}) custom-call(bf16[256,768]{1,0:T(8,128)(2,1)S(1)} %get-tuple-element.134.refs_0_, bf16[256,384]{1,0:T(8,128)(2,1)S(1)} %get-tuple-element.135.refs_1_, bf16[256,768]{1,0:T(8,128)(2,1)S(1)} %get-tuple-element.136.refs_2_, ...), custom_call_target="tpu_custom_call" | custom-call | flops 603979776 | bytes 3932160 | tf_op jit(solution)/shard_map/pallas_call | solution.py:336
  74.1 1.5 shard_map.344
  75.6 1.4 collective-permute-start.21
  77.0 1.1 shard_map.339
  78.7 1.0 shard_map.334
  79.7 0.8 copy-done.25
  80.5 1.4 collective-permute-start.13
  82.0 1.5 collective-permute-start.5
  83.5 1.0 copy-done.28
  84.5 1.4 shard_map.327
  87.2 6.2 %shard_map.332 = f32[6,32]{1,0:T(8,128)S(1)} custom-call(f32[6,256,256]{2,1,0:T(8,128)S(1)} %copy-done.6, s32[256,256]{1,0:T(8,128)S(1)} %copy-done.41), custom_call_target="tpu_custom_call" | custom-call | bytes 1835776 | tf_op jit(solution)/shard_map/pallas_call | solution.py:336
  94.0 1.9 %shard_map.330 = (f32[128,768]{1,0:T(8,128)}, f32[1,768]{1,0:T(1,128)S(1)}) custom-call(bf16[256,768]{1,0:T(8,128)(2,1)S(1)} %copy-done.9, f32[128,768]{1,0:T(8,128)S(1)} %copy-done.33, f32[128,768]{1,0:T(8,128)S(1)} %copy-done.35, bf16[128,768]{1,0:T(8,128)(2,1)} %collective-permute-done.5.got, f32[1,768]{1,0:T(1,128)S(1)} %reshape.63.gain), custom_call_target="tpu_custom_call" | custom-call | bytes 1775616 | tf_op jit(solution)/shard_map/pallas_call | solution.py:336
  96.0 8.8 %collective-permute-done.21.got = bf16[192,3072]{1,0:T(8,128)(2,1)} collective-permute-done((bf16[192,3072]{1,0:T(8,128)(2,1)}, bf16[192,3072]{1,0:T(8,128)(2,1)}, u32[]{:S(2)}, u32[]{:S(2)}) %collective-permute-start.21) | collective-permute-done | bytes 1179680 | tf_op jit(solution)/shard_map/ppermute | solution.py:381
  104.7 2.3 %shard_map.345 = (bf16[96,3072]{1,0:T(8,128)(2,1)S(1)}, bf16[96,3072]{1,0:T(8,128)(2,1)}) custom-call(bf16[192,3072]{1,0:T(8,128)(2,1)S(1)} %copy-done.14, bf16[192,3072]{1,0:T(8,128)(2,1)} %collective-permute-done.21.got), custom_call_target="tpu_custom_call" | custom-call | bytes 3538944 | tf_op jit(solution)/shard_map/pallas_call | solution.py:336
  107.1 1.5 collective-permute-start.22
  108.6 1.3 constant_dynamic-update-slice_fusion.1
  109.9 7.4 %collective-permute-done.17.got = bf16[192,1536]{1,0:T(8,128)(2,1)} collective-permute-done((bf16[192,1536]{1,0:T(8,128)(2,1)}, bf16[192,1536]{1,0:T(8,128)(2,1)}, u32[]{:S(2)}, u32[]{:S(2)}) %collective-permute-start.17) | collective-permute-done | bytes 589856 | tf_op jit(solution)/shard_map/ppermute | solution.py:381
  117.4 1.1 copy-done.24
  118.4 1.9 %shard_map.340 = (bf16[96,1536]{1,0:T(8,128)(2,1)S(1)}, bf16[96,1536]{1,0:T(8,128)(2,1)}) custom-call(bf16[192,1536]{1,0:T(8,128)(2,1)S(1)} %copy-done.24, bf16[192,1536]{1,0:T(8,128)(2,1)} %collective-permute-done.17.got), custom_call_target="tpu_custom_call" | custom-call | bytes 1769472 | tf_op jit(solution)/shard_map/pallas_call | solution.py:336
  121.1 1.5 collective-permute-start.18
  122.6 6.9 %collective-permute-done.13.got = bf16[192,1536]{1,0:T(8,128)(2,1)} collective-permute-done((bf16[192,1536]{1,0:T(8,128)(2,1)}, bf16[192,1536]{1,0:T(8,128)(2,1)}, u32[]{:S(2)}, u32[]{:S(2)}) %collective-permute-start.13) | collective-permute-done | bytes 589856 | tf_op jit(solution)/shard_map/ppermute | solution.py:381
  129.5 1.1 copy-done.26
  130.6 1.9 %shard_map.335 = (bf16[96,1536]{1,0:T(8,128)(2,1)S(1)}, bf16[96,1536]{1,0:T(8,128)(2,1)}) custom-call(bf16[192,1536]{1,0:T(8,128)(2,1)S(1)} %copy-done.26, bf16[192,1536]{1,0:T(8,128)(2,1)} %collective-permute-done.13.got), custom_call_target="tpu_custom_call" | custom-call | bytes 1769472 | tf_op jit(solution)/shard_map/pallas_call | solution.py:336
  133.1 1.5 collective-permute-start.14
  134.7 1.2 collective-permute-done.7
  135.9 1.5 collective-permute-start.8
  137.4 2.2 %collective-permute-done.8 = f32[2496]{0:T(1024)S(1)} collective-permute-done((f32[2496]{0:T(1024)S(1)}, f32[2496]{0:T(1024)S(1)}, u32[]{:S(2)}, u32[]{:S(2)}) %collective-permute-start.8) | collective-permute-done | bytes 10016 | tf_op jit(solution)/shard_map/ppermute | solution.py:404
  140.1 0.9 copy-done.45
  141.1 1.4 shard_map.331
  142.4 0.9 collective-permute-done.9
  143.3 1.5 collective-permute-start.6
  144.8 2.6 %collective-permute-start.10 = (f32[2496]{0:T(1024)S(1)}, f32[2496]{0:T(1024)S(1)}, u32[]{:S(2)}, u32[]{:S(2)}) collective-permute-start(f32[2496]{0:T(1024)S(1)} %add.25), channel_id=1, source_target_pairs={{0,16},{2,18},{4,20},{6,22},{8,24},{10,26},{12,28},{14,30},{16,0},... | collective-permute-start | bytes 29960 | tf_op jit(solution)/shard_map/ppermute | solution.py:404
  147.4 1.6 add_convert_fusion
  150.0 1.0 copy-done.37
  151.0 1.0 shard_map.341
  152.0 2.7 %collective-permute-start.19 = (bf16[48,1536]{1,0:T(8,128)(2,1)S(1)}, bf16[48,1536]{1,0:T(8,128)(2,1)S(1)}, u32[]{:S(2)}, u32[]{:S(2)}) collective-permute-start(bf16[48,1536]{1,0:T(8,128)(2,1)S(1)} %get-tuple-element.163), channel_id=1, source_target_pairs={{0,16},{2,18},{4,20},{6,22},{8,24},{10,26},{12,28},{14,30},{16,0},... | collective-permute-start | bytes 442376 | tf_op jit(solution)/shard_map/ppermute | solution.py:381
  154.7 1.0 shard_map.336
  156.3 2.7 %collective-permute-start.23 = (bf16[48,3072]{1,0:T(8,128)(2,1)S(1)}, bf16[48,3072]{1,0:T(8,128)(2,1)S(1)}, u32[]{:S(2)}, u32[]{:S(2)}) collective-permute-start(bf16[48,3072]{1,0:T(8,128)(2,1)S(1)} %get-tuple-element.178), channel_id=1, source_target_pairs={{0,16},{2,18},{4,20},{6,22},{8,24},{10,26},{12,28},{14,30},{16,0},... | collective-permute-start | bytes 884744 | tf_op jit(solution)/shard_map/ppermute | solution.py:381
  158.9 0.8 convert_add_fusion
  161.0 9.7 %collective-permute-done.19.got = bf16[48,1536]{1,0:T(8,128)(2,1)S(1)} collective-permute-done((bf16[48,1536]{1,0:T(8,128)(2,1)S(1)}, bf16[48,1536]{1,0:T(8,128)(2,1)S(1)}, u32[]{:S(2)}, u32[]{:S(2)}) %collective-permute-start.19) | collective-permute-done | bytes 147488 | tf_op jit(solution)/shard_map/ppermute | solution.py:381
  171.5 2.4 %collective-permute-done.15.got = bf16[48,1536]{1,0:T(8,128)(2,1)S(1)} collective-permute-done((bf16[48,1536]{1,0:T(8,128)(2,1)S(1)}, bf16[48,1536]{1,0:T(8,128)(2,1)S(1)}, u32[]{:S(2)}, u32[]{:S(2)}) %collective-permute-start.15) | collective-permute-done | bytes 147488 | tf_op jit(solution)/shard_map/ppermute | solution.py:381
  174.6 3.8 %collective-permute-done.23.got = bf16[48,3072]{1,0:T(8,128)(2,1)S(1)} collective-permute-done((bf16[48,3072]{1,0:T(8,128)(2,1)S(1)}, bf16[48,3072]{1,0:T(8,128)(2,1)S(1)}, u32[]{:S(2)}, u32[]{:S(2)}) %collective-permute-start.23) | collective-permute-done | bytes 294944 | tf_op jit(solution)/shard_map/ppermute | solution.py:381
  178.5 0.8 shard_map.347
  (132 shorter events, 11.7 us)
Async XLA Ops:
  2.3 1.1 copy-start.15
  3.4 1.1 copy-start.17
  4.5 1.1 copy-start.19
  8.2 6.4 %copy-start.48 = (f32[768]{0:T(1024)S(1)}, f32[768]{0:T(1024)}, u32[]{:S(2)}) copy-start(f32[768]{0:T(1024)} %param.24) | copy-start | bytes 9220
  8.2 6.4 %copy-start.3 = (bf16[768,384]{1,0:T(8,128)(2,1)S(1)}, bf16[768,384]{1,0:T(8,128)(2,1)}, u32[]{:S(2)}) copy-start(bf16[768,384]{1,0:T(8,128)(2,1)} %ck.3) | copy-start | bytes 1769476
  8.2 6.4 %copy-start.4 = (bf16[768,384]{1,0:T(8,128)(2,1)S(1)}, bf16[768,384]{1,0:T(8,128)(2,1)}, u32[]{:S(2)}) copy-start(bf16[768,384]{1,0:T(8,128)(2,1)} %cv.3) | copy-start | bytes 1769476
  8.2 6.4 %copy-start.31 = (bf16[256,768]{1,0:T(8,128)(2,1)S(1)}, bf16[256,768]{1,0:T(8,128)(2,1)}, u32[]{:S(2)}) copy-start(bf16[256,768]{1,0:T(8,128)(2,1)} %refs_4_.1) | copy-start | bytes 1179652
  11.5 12.2 %copy-start.1 = (bf16[768,384]{1,0:T(8,128)(2,1)S(1)}, bf16[768,384]{1,0:T(8,128)(2,1)}, u32[]{:S(2)}) copy-start(bf16[768,384]{1,0:T(8,128)(2,1)} %cq.3) | copy-start | bytes 1769476
  11.5 12.2 %copy-start.2 = (bf16[384,768]{1,0:T(8,128)(2,1)S(1)}, bf16[384,768]{1,0:T(8,128)(2,1)}, u32[]{:S(2)}) copy-start(bf16[384,768]{1,0:T(8,128)(2,1)} %co.3) | copy-start | bytes 1769476
  11.5 12.2 %copy-start.8 = (bf16[256,768]{1,0:T(8,128)(2,1)S(1)}, bf16[256,768]{1,0:T(8,128)(2,1)}, u32[]{:S(2)}) copy-start(bf16[256,768]{1,0:T(8,128)(2,1)} %inputs.5) | copy-start | bytes 1179652
  11.6 12.2 %collective-permute-start = (bf16[256,768]{1,0:T(8,128)(2,1)S(1)}, bf16[256,768]{1,0:T(8,128)(2,1)S(1)}, u32[]{:S(2)}, u32[]{:S(2)}) collective-permute-start(bf16[256,768]{1,0:T(8,128)(2,1)S(1)} %get-tuple-element.101), channel_id=1, source_target_pairs={{0,1},{1,0},{2,3},{3,2},{4,5},{5,4},{6,7},{7,6},{8,9},{9,8},{10,11... | collective-permute-start | bytes 1179656 | tf_op jit(solution)/shard_map/ppermute | solution.py:350
  14.7 13.1 %copy-start.49 = (f32[768]{0:T(1024)S(1)}, f32[768]{0:T(1024)}, u32[]{:S(2)}) copy-start(f32[768]{0:T(1024)} %param.25) | copy-start | bytes 9220
  14.7 13.1 %copy-start.12 = (bf16[256,768]{1,0:T(8,128)(2,1)S(1)}, bf16[256,768]{1,0:T(8,128)(2,1)}, u32[]{:S(2)}) copy-start(bf16[256,768]{1,0:T(8,128)(2,1)} %refs_0_.1) | copy-start | bytes 1179652
  23.7 4.0 %copy-start = (bf16[1024,768]{1,0:T(8,128)(2,1)S(1)}, bf16[1024,768]{1,0:T(8,128)(2,1)}, u32[]{:S(2)}) copy-start(bf16[1024,768]{1,0:T(8,128)(2,1)} %fd.3) | copy-start | bytes 4718596
  23.8 12.5 %copy-start.11 = (bf16[768,1024]{1,0:T(8,128)(2,1)S(1)}, bf16[768,1024]{1,0:T(8,128)(2,1)}, u32[]{:S(2)}) copy-start(bf16[768,1024]{1,0:T(8,128)(2,1)} %fu.1) | copy-start | bytes 4718596
  25.9 10.4 %copy-start.10 = (bf16[768,1024]{1,0:T(8,128)(2,1)S(1)}, bf16[768,1024]{1,0:T(8,128)(2,1)}, u32[]{:S(2)}) copy-start(bf16[768,1024]{1,0:T(8,128)(2,1)} %fg.1) | copy-start | bytes 4718596
  25.9 10.3 %collective-permute-start.1 = (bf16[256,768]{1,0:T(8,128)(2,1)S(1)}, bf16[256,768]{1,0:T(8,128)(2,1)S(1)}, u32[]{:S(2)}, u32[]{:S(2)}) collective-permute-start(bf16[256,768]{1,0:T(8,128)(2,1)S(1)} %get-tuple-element.106), channel_id=1, source_target_pairs={{0,1},{1,0},{2,3},{3,2},{4,5},{5,4},{6,7},{7,6},{8,9},{9,8},{10,11... | collective-permute-start | bytes 1179656 | tf_op jit(solution)/shard_map/ppermute | solution.py:350
  39.0 3.5 %copy-start.27 = (bf16[256,1024]{1,0:T(8,128)(2,1)}, bf16[256,1024]{1,0:T(8,128)(2,1)S(1)}, u32[]{:S(2)}) copy-start(bf16[256,1024]{1,0:T(8,128)(2,1)S(1)} %get-tuple-element.107.hidden.refs_1_) | copy-start | bytes 1572868
  42.5 31.6 %collective-permute-start.20 = (bf16[384,3072]{1,0:T(8,128)(2,1)S(1)}, bf16[384,3072]{1,0:T(8,128)(2,1)S(1)}, u32[]{:S(2)}, u32[]{:S(2)}) collective-permute-start(bf16[384,3072]{1,0:T(8,128)(2,1)S(1)} %get-tuple-element.172), channel_id=1, source_target_pairs={{0,2},{2,0},{4,6},{6,4},{8,10},{10,8},{12,14},{14,12},{16,18},{18,... | collective-permute-start | bytes 7077896 | tf_op jit(solution)/shard_map/ppermute | solution.py:381
  42.6 11.5 %collective-permute-start.3 = (bf16[256,768]{1,0:T(8,128)(2,1)S(1)}, bf16[256,768]{1,0:T(8,128)(2,1)S(1)}, u32[]{:S(2)}, u32[]{:S(2)}) collective-permute-start(bf16[256,768]{1,0:T(8,128)(2,1)S(1)} %get-tuple-element.112), channel_id=1, source_target_pairs={{0,1},{1,0},{2,3},{3,2},{4,5},{5,4},{6,7},{7,6},{8,9},{9,8},{10,11... | collective-permute-start | bytes 1179656 | tf_op jit(solution)/shard_map/ppermute | solution.py:350
  54.1 13.6 %copy-start.22 = (bf16[384,768]{1,0:T(8,128)(2,1)S(1)}, bf16[384,768]{1,0:T(8,128)(2,1)}, u32[]{:S(2)}) copy-start(bf16[384,768]{1,0:T(8,128)(2,1)} %so.3) | copy-start | bytes 1769476
  57.0 15.0 %copy-start.42 = (bf16[256,384]{1,0:T(8,128)(2,1)}, bf16[256,384]{1,0:T(8,128)(2,1)S(1)}, u32[]{:S(2)}) copy-start(bf16[256,384]{1,0:T(8,128)(2,1)S(1)} %get-tuple-element.126.dk.refs_5_) | copy-start | bytes 589828
  57.0 15.0 %copy-start.44 = (bf16[256,384]{1,0:T(8,128)(2,1)}, bf16[256,384]{1,0:T(8,128)(2,1)S(1)}, u32[]{:S(2)}) copy-start(bf16[256,384]{1,0:T(8,128)(2,1)S(1)} %get-tuple-element.127.dv.refs_6_) | copy-start | bytes 589828
  57.0 10.7 %copy-start.16 = (bf16[768,384]{1,0:T(8,128)(2,1)S(1)}, bf16[768,384]{1,0:T(8,128)(2,1)}, u32[]{:S(2)}) copy-start(bf16[768,384]{1,0:T(8,128)(2,1)} %sq.3) | copy-start | bytes 1769476
  57.0 10.7 %copy-start.18 = (bf16[768,384]{1,0:T(8,128)(2,1)S(1)}, bf16[768,384]{1,0:T(8,128)(2,1)}, u32[]{:S(2)}) copy-start(bf16[768,384]{1,0:T(8,128)(2,1)} %sk.3) | copy-start | bytes 1769476
  57.0 10.7 %copy-start.20 = (bf16[768,384]{1,0:T(8,128)(2,1)S(1)}, bf16[768,384]{1,0:T(8,128)(2,1)}, u32[]{:S(2)}) copy-start(bf16[768,384]{1,0:T(8,128)(2,1)} %sv.3) | copy-start | bytes 1769476
  57.0 10.7 %collective-permute-start.4 = (bf16[256,768]{1,0:T(8,128)(2,1)S(1)}, bf16[256,768]{1,0:T(8,128)(2,1)S(1)}, u32[]{:S(2)}, u32[]{:S(2)}) collective-permute-start(bf16[256,768]{1,0:T(8,128)(2,1)S(1)} %get-tuple-element.117), channel_id=1, source_target_pairs={{0,1},{1,0},{2,3},{3,2},{4,5},{5,4},{6,7},{7,6},{8,9},{9,8},{10,11... | collective-permute-start | bytes 1179656 | tf_op jit(solution)/shard_map/ppermute | solution.py:350
  60.6 16.4 %collective-permute-start.16 = (bf16[384,1536]{1,0:T(8,128)(2,1)S(1)}, bf16[384,1536]{1,0:T(8,128)(2,1)S(1)}, u32[]{:S(2)}, u32[]{:S(2)}) collective-permute-start(bf16[384,1536]{1,0:T(8,128)(2,1)S(1)} %get-tuple-element.157), channel_id=1, source_target_pairs={{0,2},{2,0},{4,6},{6,4},{8,10},{10,8},{12,14},{14,12},{16,18},{18,... | collective-permute-start | bytes 3538952 | tf_op jit(solution)/shard_map/ppermute | solution.py:381
  72.0 2.1 %copy-start.32 = (f32[128,768]{1,0:T(8,128)}, f32[128,768]{1,0:T(8,128)S(1)}, u32[]{:S(2)}) copy-start(f32[128,768]{1,0:T(8,128)S(1)} %get-tuple-element.122.dfirst) | copy-start | bytes 1179652
  72.0 3.6 %copy-start.5 = (f32[6,256,256]{2,1,0:T(8,128)}, f32[6,256,256]{2,1,0:T(8,128)S(1)}, u32[]{:S(2)}) copy-start(f32[6,256,256]{2,1,0:T(8,128)S(1)} %get-tuple-element.133.dscore) | copy-start | bytes 4718596
  72.0 3.6 %copy-start.34 = (f32[128,768]{1,0:T(8,128)}, f32[128,768]{1,0:T(8,128)S(1)}, u32[]{:S(2)}) copy-start(f32[128,768]{1,0:T(8,128)S(1)} %get-tuple-element.123.kept) | copy-start | bytes 1179652
  74.0 4.7 %collective-permute-start.12 = (bf16[384,1536]{1,0:T(8,128)(2,1)S(1)}, bf16[384,1536]{1,0:T(8,128)(2,1)S(1)}, u32[]{:S(2)}, u32[]{:S(2)}) collective-permute-start(bf16[384,1536]{1,0:T(8,128)(2,1)S(1)} %get-tuple-element.141), channel_id=1, source_target_pairs={{0,2},{2,0},{4,6},{6,4},{8,10},{10,8},{12,14},{14,12},{16,18},{18,... | collective-permute-start | bytes 3538952 | tf_op jit(solution)/shard_map/ppermute | solution.py:381
  75.6 4.1 %copy-start.13 = (bf16[192,3072]{1,0:T(8,128)(2,1)}, bf16[192,3072]{1,0:T(8,128)(2,1)S(1)}, u32[]{:S(2)}) copy-start(bf16[192,3072]{1,0:T(8,128)(2,1)S(1)} %get-tuple-element.173.kept) | copy-start | bytes 3538948
  75.6 29.2 %collective-permute-start.21 = (bf16[192,3072]{1,0:T(8,128)(2,1)}, bf16[192,3072]{1,0:T(8,128)(2,1)}, u32[]{:S(2)}, u32[]{:S(2)}) collective-permute-start(bf16[192,3072]{1,0:T(8,128)(2,1)} %get-tuple-element.174), channel_id=1, source_target_pairs={{0,4},{2,6},{4,0},{6,2},{8,12},{10,14},{12,8},{14,10},{16,20},{18,... | collective-permute-start | bytes 3538952 | tf_op jit(solution)/shard_map/ppermute | solution.py:381
  78.1 2.4 %copy-start.23 = (bf16[192,1536]{1,0:T(8,128)(2,1)}, bf16[192,1536]{1,0:T(8,128)(2,1)S(1)}, u32[]{:S(2)}) copy-start(bf16[192,1536]{1,0:T(8,128)(2,1)S(1)} %get-tuple-element.158.kept) | copy-start | bytes 1769476
  78.1 39.3 %collective-permute-start.17 = (bf16[192,1536]{1,0:T(8,128)(2,1)}, bf16[192,1536]{1,0:T(8,128)(2,1)}, u32[]{:S(2)}, u32[]{:S(2)}) collective-permute-start(bf16[192,1536]{1,0:T(8,128)(2,1)} %get-tuple-element.159), channel_id=1, source_target_pairs={{0,4},{2,6},{4,0},{6,2},{8,12},{10,14},{12,8},{14,10},{16,20},{18,... | collective-permute-start | bytes 1769480 | tf_op jit(solution)/shard_map/ppermute | solution.py:381
  80.5 49.0 %collective-permute-start.13 = (bf16[192,1536]{1,0:T(8,128)(2,1)}, bf16[192,1536]{1,0:T(8,128)(2,1)}, u32[]{:S(2)}, u32[]{:S(2)}) collective-permute-start(bf16[192,1536]{1,0:T(8,128)(2,1)} %get-tuple-element.143), channel_id=1, source_target_pairs={{0,4},{2,6},{4,0},{6,2},{8,12},{10,14},{12,8},{14,10},{16,20},{18,... | collective-permute-start | bytes 1769480 | tf_op jit(solution)/shard_map/ppermute | solution.py:381
  82.0 12.1 %collective-permute-start.5 = (bf16[128,768]{1,0:T(8,128)(2,1)}, bf16[128,768]{1,0:T(8,128)(2,1)}, u32[]{:S(2)}, u32[]{:S(2)}) collective-permute-start(bf16[128,768]{1,0:T(8,128)(2,1)} %get-tuple-element.124), channel_id=1, source_target_pairs={{0,1},{1,0},{2,3},{3,2},{4,5},{5,4},{6,7},{7,6},{8,9},{9,8},{10,11... | collective-permute-start | bytes 589832 | tf_op jit(solution)/shard_map/ppermute | solution.py:350
  84.5 2.6 %copy-start.6 = (f32[6,256,256]{2,1,0:T(8,128)S(1)}, f32[6,256,256]{2,1,0:T(8,128)}, u32[]{:S(2)}) copy-start(f32[6,256,256]{2,1,0:T(8,128)} %copy-done.5) | copy-start | bytes 4718596
  84.5 2.6 %copy-start.41 = (s32[256,256]{1,0:T(8,128)S(1)}, s32[256,256]{1,0:T(8,128)}, u32[]{:S(2)}) copy-start(s32[256,256]{1,0:T(8,128)} %buckets.3) | copy-start | bytes 786436
  86.6 7.4 %copy-start.9 = (bf16[256,768]{1,0:T(8,128)(2,1)S(1)}, bf16[256,768]{1,0:T(8,128)(2,1)}, u32[]{:S(2)}) copy-start(bf16[256,768]{1,0:T(8,128)(2,1)} %inputs.5) | copy-start | bytes 1179652
  86.6 7.4 %copy-start.33 = (f32[128,768]{1,0:T(8,128)S(1)}, f32[128,768]{1,0:T(8,128)}, u32[]{:S(2)}) copy-start(f32[128,768]{1,0:T(8,128)} %copy-done.32) | copy-start | bytes 1179652
  86.6 7.4 %copy-start.35 = (f32[128,768]{1,0:T(8,128)S(1)}, f32[128,768]{1,0:T(8,128)}, u32[]{:S(2)}) copy-start(f32[128,768]{1,0:T(8,128)} %copy-done.34) | copy-start | bytes 1179652
  86.6 58.2 %collective-permute-start.2 = (bf16[128,768]{1,0:T(8,128)(2,1)}, bf16[128,768]{1,0:T(8,128)(2,1)}, u32[]{:S(2)}, u32[]{:S(2)}) collective-permute-start(bf16[128,768]{1,0:T(8,128)(2,1)} %get-tuple-element.110), channel_id=1, source_target_pairs={{0,1},{1,0},{2,3},{3,2},{4,5},{5,4},{6,7},{7,6},{8,9},{9,8},{10,11... | collective-permute-start | bytes 589832 | tf_op jit(solution)/shard_map/ppermute | solution.py:350
  87.1 17.6 %copy-start.14 = (bf16[192,3072]{1,0:T(8,128)(2,1)S(1)}, bf16[192,3072]{1,0:T(8,128)(2,1)}, u32[]{:S(2)}) copy-start(bf16[192,3072]{1,0:T(8,128)(2,1)} %copy-done.13) | copy-start | bytes 3538948
  104.7 35.4 %copy-start.43 = (bf16[256,384]{1,0:T(8,128)(2,1)S(1)}, bf16[256,384]{1,0:T(8,128)(2,1)}, u32[]{:S(2)}) copy-start(bf16[256,384]{1,0:T(8,128)(2,1)} %copy-done.42) | copy-start | bytes 589828
  107.1 27.6 %copy-start.50 = (f32[192]{0:T(256)S(1)}, f32[192]{0:T(256)}, u32[]{:S(2)}) copy-start(f32[192]{0:T(256)} %reshape.67) | copy-start | bytes 2308
  107.1 49.1 %collective-permute-start.22 = (bf16[96,3072]{1,0:T(8,128)(2,1)}, bf16[96,3072]{1,0:T(8,128)(2,1)S(1)}, u32[]{:S(2)}, u32[]{:S(2)}) collective-permute-start(bf16[96,3072]{1,0:T(8,128)(2,1)} %get-tuple-element.176), channel_id=1, source_target_pairs={{0,8},{2,10},{4,12},{6,14},{8,0},{10,2},{12,4},{14,6},{16,24},{18,... | collective-permute-start | bytes 1769480 | tf_op jit(solution)/shard_map/ppermute | solution.py:381
  117.4 1.1 copy-start.24
  118.4 16.2 %copy-start.47 = (f32[2496]{0:T(1024)S(1)}, f32[2496]{0:T(1024)}, u32[]{:S(2)}) copy-start(f32[2496]{0:T(1024)} %constant_dynamic-update-slice_fusion.1) | copy-start | bytes 29956
  118.4 29.0 %copy-start.30 = (f32[128,768]{1,0:T(8,128)S(1)}, f32[128,768]{1,0:T(8,128)}, u32[]{:S(2)}) copy-start(f32[128,768]{1,0:T(8,128)} %copy-done.29) | copy-start | bytes 1179652
  121.1 29.0 %collective-permute-start.18 = (bf16[96,1536]{1,0:T(8,128)(2,1)}, bf16[96,1536]{1,0:T(8,128)(2,1)}, u32[]{:S(2)}, u32[]{:S(2)}) collective-permute-start(bf16[96,1536]{1,0:T(8,128)(2,1)} %get-tuple-element.161), channel_id=1, source_target_pairs={{0,8},{2,10},{4,12},{6,14},{8,0},{10,2},{12,4},{14,6},{16,24},{18,... | collective-permute-start | bytes 884744 | tf_op jit(solution)/shard_map/ppermute | solution.py:381
  129.5 1.1 copy-start.26
  133.1 21.6 %collective-permute-start.14 = (bf16[96,1536]{1,0:T(8,128)(2,1)}, bf16[96,1536]{1,0:T(8,128)(2,1)}, u32[]{:S(2)}, u32[]{:S(2)}) collective-permute-start(bf16[96,1536]{1,0:T(8,128)(2,1)} %get-tuple-element.145), channel_id=1, source_target_pairs={{0,8},{2,10},{4,12},{6,14},{8,0},{10,2},{12,4},{14,6},{16,24},{18,... | collective-permute-start | bytes 884744 | tf_op jit(solution)/shard_map/ppermute | solution.py:381
  134.7 1.2 collective-permute-start.7
  135.9 3.7 %collective-permute-start.8 = (f32[2496]{0:T(1024)S(1)}, f32[2496]{0:T(1024)S(1)}, u32[]{:S(2)}, u32[]{:S(2)}) collective-permute-start(f32[2496]{0:T(1024)S(1)} %add.23), channel_id=1, source_target_pairs={{0,4},{2,6},{4,0},{6,2},{8,12},{10,14},{12,8},{14,10},{16,20},{18,... | collective-permute-start | bytes 29960 | tf_op jit(solution)/shard_map/ppermute | solution.py:404
  139.6 3.7 %collective-permute-start.9 = (f32[2496]{0:T(1024)S(1)}, f32[2496]{0:T(1024)S(1)}, u32[]{:S(2)}, u32[]{:S(2)}) collective-permute-start(f32[2496]{0:T(1024)S(1)} %add.24), channel_id=1, source_target_pairs={{0,8},{2,10},{4,12},{6,14},{8,0},{10,2},{12,4},{14,6},{16,24},{18,... | collective-permute-start | bytes 29960 | tf_op jit(solution)/shard_map/ppermute | solution.py:404
  142.4 12.3 %copy-start.39 = (bf16[96,1536]{1,0:T(8,128)(2,1)S(1)}, bf16[96,1536]{1,0:T(8,128)(2,1)}, u32[]{:S(2)}) copy-start(bf16[96,1536]{1,0:T(8,128)(2,1)} %copy-done.38) | copy-start | bytes 884740
  143.3 15.6 %collective-permute-start.6 = (bf16[128,768]{1,0:T(8,128)(2,1)}, bf16[128,768]{1,0:T(8,128)(2,1)S(1)}, u32[]{:S(2)}, u32[]{:S(2)}) collective-permute-start(bf16[128,768]{1,0:T(8,128)(2,1)} %get-tuple-element.129), channel_id=1, source_target_pairs={{0,1},{1,0},{2,3},{3,2},{4,5},{5,4},{6,7},{7,6},{8,9},{9,8},{10,11... | collective-permute-start | bytes 589832 | tf_op jit(solution)/shard_map/ppermute | solution.py:350
  144.8 4.6 %collective-permute-start.10 = (f32[2496]{0:T(1024)S(1)}, f32[2496]{0:T(1024)S(1)}, u32[]{:S(2)}, u32[]{:S(2)}) collective-permute-start(f32[2496]{0:T(1024)S(1)} %add.25), channel_id=1, source_target_pairs={{0,16},{2,18},{4,20},{6,22},{8,24},{10,26},{12,28},{14,30},{16,0},... | collective-permute-start | bytes 29960 | tf_op jit(solution)/shard_map/ppermute | solution.py:404
  149.5 10.9 %collective-permute-start.11 = (f32[3,768]{1,0:T(4,128)S(1)}, f32[3,768]{1,0:T(4,128)S(1)}, u32[]{:S(2)}, u32[]{:S(2)}) collective-permute-start(f32[3,768]{1,0:T(4,128)S(1)} %reshape.68), channel_id=1, source_target_pairs={{0,1},{1,0},{2,3},{3,2},{4,5},{5,4},{6,7},{7,6},{8,9},{9,8},{10,11... | collective-permute-start | bytes 27656 | tf_op jit(solution)/shard_map/ppermute | solution.py:350
  152.0 18.7 %collective-permute-start.19 = (bf16[48,1536]{1,0:T(8,128)(2,1)S(1)}, bf16[48,1536]{1,0:T(8,128)(2,1)S(1)}, u32[]{:S(2)}, u32[]{:S(2)}) collective-permute-start(bf16[48,1536]{1,0:T(8,128)(2,1)S(1)} %get-tuple-element.163), channel_id=1, source_target_pairs={{0,16},{2,18},{4,20},{6,22},{8,24},{10,26},{12,28},{14,30},{16,0},... | collective-permute-start | bytes 442376 | tf_op jit(solution)/shard_map/ppermute | solution.py:381
  155.7 18.2 %collective-permute-start.15 = (bf16[48,1536]{1,0:T(8,128)(2,1)S(1)}, bf16[48,1536]{1,0:T(8,128)(2,1)S(1)}, u32[]{:S(2)}, u32[]{:S(2)}) collective-permute-start(bf16[48,1536]{1,0:T(8,128)(2,1)S(1)} %get-tuple-element.147), channel_id=1, source_target_pairs={{0,16},{2,18},{4,20},{6,22},{8,24},{10,26},{12,28},{14,30},{16,0},... | collective-permute-start | bytes 442376 | tf_op jit(solution)/shard_map/ppermute | solution.py:381
  156.3 22.2 %collective-permute-start.23 = (bf16[48,3072]{1,0:T(8,128)(2,1)S(1)}, bf16[48,3072]{1,0:T(8,128)(2,1)S(1)}, u32[]{:S(2)}, u32[]{:S(2)}) collective-permute-start(bf16[48,3072]{1,0:T(8,128)(2,1)S(1)} %get-tuple-element.178), channel_id=1, source_target_pairs={{0,16},{2,18},{4,20},{6,22},{8,24},{10,26},{12,28},{14,30},{16,0},... | collective-permute-start | bytes 884744 | tf_op jit(solution)/shard_map/ppermute | solution.py:381
  (11 other events, 9.6 us)
